TPU v7x, 32 devices: a whole 2x2x4 slice. The times are simulated.
32 devices in a mesh: blk: 4 (over y, core), corpus: 8 (over z, x).
Axes of the slice: x: 2, y: 2, z: 4, core: 2. Of those that a mesh axis runs over, the one named last changes fastest.
Arguments:
- states: bfloat16 [8192, 1536], P(('blk', 'corpus')), may hold values from -12 to 12
- table: bfloat16 [8192, 1536], P('corpus'), may hold values from -2.5 to 2.5
- owners: int32 [8192, 4], P(('blk', 'corpus')), may hold values from 0 to 7, as said below
- rows: int32 [8192, 4], P(('blk', 'corpus')), may hold values from 0 to 1023
Outputs:
- loss: float32 [8192], P(('blk', 'corpus'))
- state_grad: bfloat16 [8192, 1536], P(('blk', 'corpus'))
- table_grad: float32 [8192, 1536], P('corpus', 'blk')
Inputs may be any that keep to these rules, and one draw needn't show every extreme that they name: `owners`: each state names 4 different shards. Among the 256 states of one device (aligned blocks) no shard is named more than 256 times, and every device names some shard exactly 256 times.
All inputs are finite; a program needn't handle non-finite values.
Results may differ from a plain program's by a relative error of at most 0.012.
Values may be sent and summed in bfloat16 or wider, within the bound.
No kernel may reach another device: no remote copies, remote signals or barrier semaphores. Data moves between devices by JAX's collectives and lax.ppermute only.
A program may use at most 128 MiB of HBM per device.

v0:
```python
import jax
import jax.numpy as jnp
from jax import lax
from jax.experimental.layout import Layout, with_layout_constraint
from jax.sharding import PartitionSpec as P

score_scale = 0.0625
LINES = 2
LANES = 128
END_SWAP = [(0, 1), (1, 0), (2, 3), (3, 2)]
MIDDLE_SWAP = [(1, 2), (2, 1)]
OUTWARD = [(1, 0), (2, 3)]
INWARD = [(0, 1), (3, 2)]
f32 = jnp.float32
bf16 = jnp.bfloat16


def line_permute(value, pairs):
    full = [(s * LINES + i, t * LINES + i) for s, t in pairs for i in range(LINES)]
    return lax.ppermute(value, "corpus", full)


def swap(value, length, bit):
    return line_permute(value, [(a, a ^ bit) for a in range(length)])


def beside(value):
    size = lax.axis_size("corpus")
    return lax.ppermute(value, "corpus", [(c, c ^ 1) for c in range(size)])


def across(value, bit):
    size = lax.axis_size("blk")
    return lax.ppermute(value, "blk", [(b, b ^ bit) for b in range(size)])


def blk_gather(value):
    size = lax.axis_size("blk")
    out = {0: value}
    bit = size // 2
    while bit:
        out.update({k | bit: across(v, bit) for k, v in out.items()})
        bit //= 2
    return [out[k] for k in range(size)]


def turned(value, k, size):
    step = value.shape[0] // size
    return [value[(j ^ k) * step : ((j ^ k) + 1) * step] for j in range(size)]


def rowwise(value):
    return with_layout_constraint(value, Layout(major_to_minor=(0, 1)))


def apart(value):
    return lax.optimization_barrier(value)


def after(value, *earlier):
    return lax.optimization_barrier((value, *earlier))[0]


def local(states, table, owners, rows):
    state_rows, width = states.shape
    top = owners.shape[1]
    shard_rows = table.shape[0]
    blks = lax.axis_size("blk")
    length = lax.axis_size("corpus") // LINES
    b = lax.axis_index("blk")
    a = lax.axis_index("corpus") // LINES
    lane = lax.axis_index("corpus") % LINES
    part = width // blks
    short = length == 4
    widths = [LANES, part - LANES] if short and part > LANES else [part]
    chunks = len(widths)
    group = blks * state_rows
    starts = [sum(widths[:k]) for k in range(chunks)]
    cols = [slice(at, at + wide) for at, wide in zip(starts, widths)]

    mine = lax.dynamic_slice_in_dim(table, b * part, part, axis=1)
    ids = (owners * shard_rows + rows).astype(jnp.int32).T
    fresh = states
    if short:
        middle = (a == 1) | (a == 2)
        lead = line_permute(mine[:, : widths[0]], END_SWAP)
        beyond = line_permute(mine, MIDDLE_SWAP)
        trail = line_permute(mine[:, widths[0] :], END_SWAP)
        ids, fresh = lax.optimization_barrier((ids, states, lead))[:2]
        lead_last = line_permute(lead, MIDDLE_SWAP)
        trail_last = line_permute(trail, MIDDLE_SWAP)
        outer = line_permute(beyond, OUTWARD)
        third = jnp.where(middle, beyond, outer)
        beside_rows = jnp.concatenate([lead, after(trail, beyond)], axis=1)
        early = [mine, beside_rows, third]
        wait = [beyond]
        late, moved = [], []
        for k in range(chunks):
            piece = trail_last[:, starts[k] - widths[0] :][:, : widths[k]] if k else lead_last
            if k:
                piece = after(piece, outer, *moved[: k - 1])
            moved.append(line_permute(piece, OUTWARD))
            late.append((piece, moved[k]))
        places = [a, a ^ 1, jnp.where(a < 2, 2, 1), jnp.where(a < 2, 3, 0)]
    else:
        held, bit = mine, 1
        while bit < length:
            held = jnp.concatenate([held, swap(held, length, bit)], axis=0)
            bit *= 2
        early = [held[j * shard_rows : (j + 1) * shard_rows] for j in range(length)]
        late, wait = [], []
        places = [a ^ j for j in range(length)]

    ids = jnp.concatenate(blk_gather(ids), axis=1)
    ids = jnp.concatenate([ids, beside(ids)], axis=1)
    near = []
    for q in range(blks):
        piece = lax.dynamic_slice_in_dim(fresh, (b ^ q) * part, part, axis=1)
        near.append(across(piece, q) if q else piece)
    near = jnp.concatenate(near, axis=0)
    pair_states = jnp.concatenate([near, beside(near)], axis=0)
    bit = blks // 2
    met = across(after(states, near, *wait), bit)
    group_states = {0: states, bit: met}
    while bit > 1:
        bit //= 2
        group_states.update({k | bit: across(after(v, met), bit) for k, v in group_states.items()})
    group_states = jnp.concatenate([group_states[k] for k in range(blks)], axis=0)
    sliced = [
        lax.dynamic_slice_in_dim(group_states, (b ^ q) * part, part, axis=1) for q in range(blks)
    ]

    match, row_of = [], []
    for place in places:
        base = (place * LINES + lane) * shard_rows
        inside = (ids >= base) & (ids < base + shard_rows)
        match.append(inside)
        row_of.append(jnp.sum(jnp.where(inside, ids - base + 1, 0), axis=0) - 1)
    order = jnp.arange(shard_rows, dtype=jnp.int32)

    def pick(j, rows):
        hot = (row_of[j][:, None] == order[None, :]).astype(bf16)
        return jnp.dot(hot, rows, preferred_element_type=f32).astype(bf16)

    def choose(j, got, positive):
        return jnp.where(match[j][0][:, None], got, positive)

    def dots_of(j, got, cut):
        dots = jnp.sum(cut.astype(f32) * got.astype(f32), axis=1)
        return jnp.where(match[j], dots[None, :], 0.0)

    picked = [pick(j, rows) for j, rows in enumerate(early)]
    positive = jnp.zeros((2 * group, part), bf16)
    hard = 0.0
    for j, got in enumerate(picked):
        positive = choose(j, got, positive)
        hard = hard + dots_of(j, got, pair_states)
    bases = [positive]
    if late:
        bases = apart([positive[:, c] for c in cols])
    positives, last, came, gathered = [], [], [], []
    for k in range(chunks):
        base, gates = bases[k], ([] if k else [met])
        if late:
            j = len(early)
            piece, swapped, base = lax.optimization_barrier((*late[k], base, *gates))[:3]
            last.append(apart(pick(j, jnp.where(middle, piece, swapped))))
            base = choose(j, last[k], base)
            hard = hard + dots_of(j, last[k], pair_states[:, cols[k]])
        near_rows, away = apart((base[:group], base[group:]))
        came.append(beside(after(away, came[-1]) if came else away))
        positives.append(near_rows + came[-1])
        gathered.append(blk_gather(positives[-1]))
    half = blks // 2
    hard = hard[:, :group] + beside(after(hard[:, group:], gathered[0][half]))
    bit = half
    while bit:
        if bit == half:
            hard = after(hard, gathered[max(0, chunks - 2)][half])
        other = across(hard, bit)
        step = state_rows
        hard = hard + jnp.concatenate(
            [other[:, (q ^ bit) * step : ((q ^ bit) + 1) * step] for q in range(blks)], axis=1
        )
        bit //= 2
    hard_weight = jnp.exp(score_scale * hard).astype(bf16).astype(f32)
    hard_weight = jnp.where(jnp.arange(top)[:, None] >= 1, hard_weight, 0.0)

    score = jnp.zeros((group, group), f32)
    keys = []
    for k in range(chunks):
        full = jnp.concatenate(
            [jnp.concatenate(turned(v, q, blks), axis=0) for q, v in enumerate(gathered[k])], axis=1
        )
        keys.append(full)
        query = jnp.concatenate([s[:, cols[k]] for s in sliced], axis=1)
        score = score + lax.dot_general(
            full, query, (((1,), (1,)), ((), ())), preferred_element_type=f32
        )
    score = score_scale * score
    weight = jnp.exp(score).astype(bf16)
    total = jnp.sum(weight.astype(f32), axis=0) + jnp.sum(hard_weight, axis=0)
    prob = (weight.astype(f32) / total[None, :]).astype(bf16)
    hard_prob = (hard_weight / total[None, :]).astype(bf16)
    far = beside(jnp.concatenate([hard_prob.astype(f32), hard_weight], axis=0))
    far_prob, far_weight = far[:top], far[top:]
    pulled = jnp.dot(prob, near, preferred_element_type=f32)
    positive_grad = (score_scale * (pulled - near.astype(f32))).astype(bf16)
    pulls, far_pulls = [], []
    for k in range(chunks):
        pull = positive_grad[:, cols[k]]
        far_pulls.append(beside(after(pull, far) if k else pull))
        pulls.append(jnp.concatenate([pull, far_pulls[k]], axis=0))
    pair_prob = jnp.concatenate([hard_prob.astype(f32), far_prob], axis=1)
    wide = score_scale * pair_states.astype(f32)

    def share(j, pull, wide):
        scale = jnp.sum(jnp.where(match[j], pair_prob, 0.0), axis=0)
        value = jnp.where(match[j][0][:, None], pull, (scale[:, None] * wide).astype(bf16))
        hot = (order[:, None] == row_of[j][None, :]).astype(bf16)
        return jnp.dot(hot, value, preferred_element_type=f32)

    pull = jnp.concatenate(pulls, axis=1)
    if short:
        ends, crossed = [], []
        for k in range(chunks):
            end = share(3, pulls[k], wide[:, cols[k]]).astype(bf16)
            ends.append(line_permute(end, INWARD))
            both = (end.astype(f32) + ends[k].astype(f32)).astype(bf16)
            crossed.append(line_permute(both, MIDDLE_SWAP))
        third = apart(rowwise(share(2, after(pull, end), wide).astype(bf16)))
        later = after(pull, ends[-1])
        crossed = jnp.concatenate(crossed, axis=1)
        inner = line_permute(third, INWARD)
        beside_sum = apart(rowwise(share(1, later, wide).astype(bf16)))
        beside_sum = (beside_sum.astype(f32) + crossed.astype(f32)).astype(bf16)
        third = (third.astype(f32) + inner.astype(f32)).astype(bf16)
        table_grad = apart(rowwise(share(0, later, wide).astype(bf16))).astype(f32)
        gate = (beside_sum, third)
        table_grad = table_grad + line_permute(beside_sum, END_SWAP).astype(f32)
        table_grad = table_grad + line_permute(third, MIDDLE_SWAP).astype(f32)
    else:
        held = jnp.concatenate([share(j, pull, wide) for j in range(length)], axis=0)
        bit = length // 2
        while bit:
            cut = bit * shard_rows
            held = held[:cut] + swap(held[cut:].astype(bf16), length, bit).astype(f32)
            bit //= 2
        table_grad = held
        gate = ()

    both_weight = jnp.concatenate([hard_weight, far_weight], axis=1)

    def weighted(j, got):
        scale = jnp.sum(jnp.where(match[j], both_weight, 0.0), axis=0)
        return scale[:, None] * got.astype(f32)

    shares = sum(weighted(j, got) for j, got in enumerate(picked))
    if late:
        shares = shares + weighted(len(early), jnp.concatenate(last, axis=1))
    moved = after(beside(after(shares[group:].astype(bf16), far_pulls[-1])), *gate)
    shares = (shares[:group] + moved.astype(f32)).astype(bf16)
    mine_weight = weight[:, :state_rows]
    own_total = total[:state_rows]
    pieces = []
    for q in range(blks):
        piece = shares[q * state_rows : (q + 1) * state_rows]
        if q:
            piece = across(piece, q)
        key = jnp.concatenate([key[:, q * w : (q + 1) * w] for key, w in zip(keys, widths)], axis=1)
        accum = lax.dot_general(
            mine_weight, key, (((0,), (0,)), ((), ())), preferred_element_type=f32
        ) + piece.astype(f32)
        pieces.append(
            (score_scale * (accum / own_total[:, None] - key[:state_rows].astype(f32))).astype(bf16)
        )
    state_grad = jnp.zeros((state_rows, width), bf16)
    for q in range(blks):
        state_grad = lax.dynamic_update_slice_in_dim(state_grad, pieces[q], (b ^ q) * part, axis=1)
    corner = score[:state_rows, :state_rows]
    spot = jnp.arange(state_rows)
    own = jnp.sum(jnp.where(spot[:, None] == spot[None, :], corner, 0.0), axis=0)
    loss = jnp.log(own_total) - own
    return loss, state_grad, table_grad


def solution(mesh):
    return jax.shard_map(
        local,
        mesh=mesh,
        in_specs=(
            P(("blk", "corpus"), None),
            P("corpus", None),
            P(("blk", "corpus"), None),
            P(("blk", "corpus"), None),
        ),
        out_specs=(P(("blk", "corpus")), P(("blk", "corpus"), None), P("corpus", "blk")),
        check_vma=False,
    )
```

profile of v0, /device:TPU:1, one launch (start us, length us, event | category | flops | bytes accessed | tf_op | source)
XLA Modules:
  0.0 195.6 jit_solution(1563775033992547482)
XLA Ops:
  0.7 1.9 copy-done
  2.6 2.2 %collective-permute-start = (bf16[1024,128]{1,0:T(8,128)(2,1)S(1)}, bf16[1024,128]{1,0:T(8,128)(2,1)}, u32[]{:S(2)}, u32[]{:S(2)}) collective-permute-start(bf16[1024,128]{1,0:T(8,128)(2,1)S(1)} %constant_dynamic-slice_fusion.1), channel_id=1, source_target_pairs={{0,2},{1,3},{2,0},{3,1},{4,6},{5,7},{6,4},{7,5},{8,10},{9,11},{10,... | collective-permute-start | bytes 786440 | tf_op jit(solution)/shard_map/ppermute | solution.py:20
  6.6 1.6 collective-permute-start.7
  8.2 1.2 constant_dynamic-update-slice_fusion.8
  9.4 1.5 collective-permute-done
  10.9 1.1 collective-permute-start.2
  12.0 3.0 %collective-permute-start.1 = (s32[4,256]{1,0:T(4,128)S(1)}, s32[4,256]{1,0:T(4,128)S(1)}, u32[]{:S(2)}, u32[]{:S(2)}) collective-permute-start(s32[4,256]{1,0:T(4,128)S(1)} %add_bitcast_fusion), channel_id=1, source_target_pairs={{0,8},{8,0},{16,24},{24,16},{1,9},{9,1},{17,25},{25,17},{2,10},{10... | collective-permute-start | bytes 12296 | tf_op jit(solution)/shard_map/ppermute | solution.py:34
  15.0 2.3 %copy.7 = bf16[256,1536]{0,1:T(8,128)(2,1)} copy(bf16[256,1536]{1,0:T(8,128)(2,1)} %param.4) | data formatting | bytes 1572864 | tf_op jit(solution)/shard_map/optimization_barrier | solution.py:89
  17.2 1.3 constant_dynamic-update-slice_fusion.13
  18.6 1.3 collective-permute-start.11
  21.6 1.2 collective-permute-start.4
  22.8 1.7 collective-permute-done.4
  24.5 1.2 collective-permute-start.10
  25.9 3.6 %fusion.30 = bf16[2048,384]{0,1:T(8,128)(2,1)S(1)} fusion(bf16[1024,384]{1,0:T(8,128)(2,1)} %constant_dynamic-slice_fusion.14, s32[2048]{0:T(1024)S(1)} %get-tuple-element.140), kind=kOutput, calls=%fused_computation.52 | convolution fusion | flops 1613496320 | bytes 2367488 | tf_op jit(solution)/shard_map/dot_general | solution.py:143
  30.5 1.3 collective-permute-start.26
  31.8 1.3 collective-permute-start.8
  33.2 1.3 collective-permute-start.6
  35.5 3.6 %fusion.31 = bf16[2048,384]{0,1:T(8,128)(2,1)S(1)} fusion(s32[2048]{0:T(1024)S(1)} %get-tuple-element.141, bf16[1024,256]{1,0:T(8,128)(2,1)} %collective-permute-done.9, bf16[1024,128]{1,0:T(8,128)(2,1)} %collective-permute-done), kind=kOutput, calls=%fused_computation.53 | convolution fusion | flops 1615069184 | bytes 2367488 | tf_op jit(solution)/shard_map/dot_general | solution.py:143
  39.1 10.6 %collective-permute-done.26 = bf16[1024,384]{0,1:T(8,128)(2,1)S(1)} collective-permute-done((bf16[1024,384]{0,1:T(8,128)(2,1)S(1)}, bf16[1024,384]{0,1:T(8,128)(2,1)S(1)}, u32[]{:S(2)}, u32[]{:S(2)}) %collective-permute-start.26) | collective-permute-done | bytes 786464 | tf_op jit(solution)/shard_map/ppermute | solution.py:29
  49.8 4.7 %collective-permute-done.8 = bf16[1024,384]{1,0:T(8,128)(2,1)S(1)} collective-permute-done((bf16[1024,384]{1,0:T(8,128)(2,1)}, bf16[1024,384]{1,0:T(8,128)(2,1)S(1)}, u32[]{:S(2)}, u32[]{:S(2)}) %collective-permute-start.8) | collective-permute-done | bytes 786464 | tf_op jit(solution)/shard_map/ppermute | solution.py:20
  54.5 2.5 %select_select_fusion = (bf16[2048,384]{0,1:T(8,128)(2,1)S(1)}, bf16[2048,384]{0,1:T(8,128)(2,1)S(1)}) fusion(bf16[2048,384]{0,1:T(8,128)(2,1)S(1)} %fusion.31, bf16[2048,384]{0,1:T(8,128)(2,1)S(1)} %fusion.30, pred[2048]{0:T(1024)(128)(4,1)S(1)} %get-tuple-element.138, pred[2048]{0:T(1024)(128)(4,1)S(1)} %get-tuple-element.139, ...), kind=kOutput, calls=%fused_computation.104 | convolution fusion | flops 1616248832 | bytes 7878657 | tf_op jit(solution)/shard_map/dot_general | solution.py:143
  57.2 1.3 collective-permute-start.21
  58.6 1.9 collective-permute-start.18
  60.5 2.1 %fusion.34 = bf16[2048,128]{0,1:T(8,128)(2,1)S(1)} fusion(s32[2048]{0:T(1024)S(1)} %broadcast_add_fusion.3, bf16[1024,128]{1,0:T(8,128)(2,1)S(1)} %collective-permute-done.5, bf16[1024,128]{1,0:T(8,128)(2,1)S(1)} %collective-permute-done.6, pred[]{:T(512)S(6)} %or.3), kind=kOutput, calls=%fused_computation.56 | convolution fusion | flops 539361280 | bytes 1056769 | tf_op jit(solution)/shard_map/dot_general | solution.py:143
  63.1 1.4 fusion.24
  64.6 5.3 %collective-permute-done.14 = bf16[1024,128]{0,1:T(8,128)(2,1)S(1)} collective-permute-done((bf16[1024,128]{0,1:T(8,128)(2,1)S(1)}, bf16[1024,128]{0,1:T(8,128)(2,1)S(1)}, u32[]{:S(2)}, u32[]{:S(2)}) %collective-permute-start.14) | collective-permute-done | bytes 262176 | tf_op jit(solution)/shard_map/ppermute | solution.py:29
  70.3 1.9 collective-permute-start.15
  72.2 2.5 %fusion.33 = bf16[2048,256]{0,1:T(8,128)(2,1)S(1)} fusion(s32[2048]{0:T(1024)S(1)} %broadcast_add_fusion.3, bf16[1024,256]{1,0:T(8,128)(2,1)S(1)} %collective-permute-done.20, bf16[1024,256]{1,0:T(8,128)(2,1)S(1)} %collective-permute-done.21, pred[]{:T(512)S(6)} %or.3), kind=kOutput, calls=%fused_computation.55 | convolution fusion | flops 1076625408 | bytes 2105345 | tf_op jit(solution)/shard_map/dot_general | solution.py:143
  76.6 1.3 collective-permute-start.22
  79.2 2.2 %collective-permute-done.28 = f32[4,1024]{1,0:T(4,128)S(1)} collective-permute-done((f32[4,1024]{1,0:T(4,128)S(1)}, f32[4,1024]{1,0:T(4,128)S(1)}, u32[]{:S(2)}, u32[]{:S(2)}) %collective-permute-start.28) | collective-permute-done | bytes 16416 | tf_op jit(solution)/shard_map/ppermute | solution.py:34
  81.4 5.1 %collective-permute-start.17 = (bf16[1024,128]{0,1:T(8,128)(2,1)S(1)}, bf16[1024,128]{0,1:T(8,128)(2,1)S(1)}, u32[]{:S(2)}, u32[]{:S(2)}) collective-permute-start(bf16[1024,128]{0,1:T(8,128)(2,1)S(1)} %collective-permute-done.16), channel_id=1, source_target_pairs={{0,8},{8,0},{16,24},{24,16},{1,9},{9,1},{17,25},{25,17},{2,10},{10... | collective-permute-start | bytes 786440 | tf_op jit(solution)/shard_map/ppermute | solution.py:34
  86.7 1.1 collective-permute-done.29
  88.6 3.6 %collective-permute-start.23 = (bf16[1024,256]{0,1:T(8,128)(2,1)S(1)}, bf16[1024,256]{0,1:T(8,128)(2,1)S(1)}, u32[]{:S(2)}, u32[]{:S(2)}) collective-permute-start(bf16[1024,256]{0,1:T(8,128)(2,1)S(1)} %add.199), channel_id=1, source_target_pairs={{0,8},{8,0},{16,24},{24,16},{1,9},{9,1},{17,25},{25,17},{2,10},{10... | collective-permute-start | bytes 1572872 | tf_op jit(solution)/shard_map/ppermute | solution.py:34
  92.4 6.2 %collective-permute-done.24 = bf16[1024,256]{0,1:T(8,128)(2,1)S(1)} collective-permute-done((bf16[1024,256]{0,1:T(8,128)(2,1)S(1)}, bf16[1024,256]{0,1:T(8,128)(2,1)S(1)}, u32[]{:S(2)}, u32[]{:S(2)}) %collective-permute-start.24) | collective-permute-done | bytes 524320 | tf_op jit(solution)/shard_map/ppermute | solution.py:34
  98.6 4.0 %collective-permute-start.25 = (bf16[1024,256]{0,1:T(8,128)(2,1)S(1)}, bf16[1024,256]{0,1:T(8,128)(2,1)S(1)}, u32[]{:S(2)}, u32[]{:S(2)}) collective-permute-start(bf16[1024,256]{0,1:T(8,128)(2,1)S(1)} %collective-permute-done.24), channel_id=1, source_target_pairs={{0,8},{8,0},{16,24},{24,16},{1,9},{9,1},{17,25},{25,17},{2,10},{10... | collective-permute-start | bytes 1572872 | tf_op jit(solution)/shard_map/ppermute | solution.py:34
  102.9 1.3 collective-permute-done.25
  104.2 2.4 %fusion.36 = f32[1024,1024]{1,0:T(8,128)S(1)} fusion(bf16[256,256]{0,1:T(8,128)(2,1)S(1)} %get-tuple-element.106, bf16[256,256]{0,1:T(8,128)(2,1)S(1)} %get-tuple-element.107, bf16[256,256]{0,1:T(8,128)(2,1)S(1)} %get-tuple-element.108, bf16[256,256]{0,1:T(8,128)(2,1)S(1)} %get-tuple-element.105, bf16[512,256]{0,1:T(8,128)(2,1)S(1)} %get-tuple-element.104, ...), kind=kOutput, calls=%fused_computation.59 | convolution fusion | flops 2178940928 | bytes 8388608 | tf_op jit(solution)/shard_map/dot_general | solution.py:197
  106.7 1.7 convert_reduce_fusion
  112.7 1.4 fusion.23
  114.1 4.1 %collective-permute-done.33 = bf16[1024,128]{0,1:T(8,128)(2,1)S(1)} collective-permute-done((bf16[1024,128]{0,1:T(8,128)(2,1)S(1)}, bf16[1024,128]{0,1:T(8,128)(2,1)S(1)}, u32[]{:S(2)}, u32[]{:S(2)}) %collective-permute-start.33) | collective-permute-done | bytes 262176 | tf_op jit(solution)/shard_map/ppermute | solution.py:29
  118.3 1.6 fusion.92
  119.8 7.8 %collective-permute-start.35 = (bf16[1024,128]{1,0:T(8,128)(2,1)S(1)}, bf16[1024,128]{1,0:T(8,128)(2,1)S(1)}, u32[]{:S(2)}, u32[]{:S(2)}) collective-permute-start(bf16[1024,128]{1,0:T(8,128)(2,1)S(1)} %fusion.92), channel_id=1, source_target_pairs={{0,2},{1,3},{6,4},{7,5},{8,10},{9,11},{14,12},{15,13},{16,18},{17,... | collective-permute-start | bytes 786440 | tf_op jit(solution)/shard_map/ppermute | solution.py:20
  127.7 3.1 %collective-permute-done.35 = bf16[1024,128]{1,0:T(8,128)(2,1)S(1)} collective-permute-done((bf16[1024,128]{1,0:T(8,128)(2,1)S(1)}, bf16[1024,128]{1,0:T(8,128)(2,1)S(1)}, u32[]{:S(2)}, u32[]{:S(2)}) %collective-permute-start.35) | collective-permute-done | bytes 262176 | tf_op jit(solution)/shard_map/ppermute | solution.py:20
  131.9 1.7 fusion.91
  133.6 5.5 %collective-permute-start.34 = (bf16[1024,256]{1,0:T(8,128)(2,1)S(1)}, bf16[1024,256]{1,0:T(8,128)(2,1)S(1)}, u32[]{:S(2)}, u32[]{:S(2)}) collective-permute-start(bf16[1024,256]{1,0:T(8,128)(2,1)S(1)} %fusion.91), channel_id=1, source_target_pairs={{0,2},{1,3},{6,4},{7,5},{8,10},{9,11},{14,12},{15,13},{16,18},{17,... | collective-permute-start | bytes 1572872 | tf_op jit(solution)/shard_map/ppermute | solution.py:20
  139.3 2.4 %fusion.85 = bf16[1024,384]{1,0:T(8,128)(2,1)S(1)} fusion(bf16[2048,384]{0,1:T(8,128)(2,1)S(1)} %maximum_maximum_fusion, bf16[2048,384]{0,1:T(8,128)(2,1)S(1)} %constant_dynamic-update-slice_fusion.9, f32[2048]{0:T(1024)S(1)} %broadcast_multiply_fusion.1, pred[2048]{0:T(1024)(128)(4,1)S(1)} %slice_reduce_fusion.2, s32[2048]{0:T(1024)S(1)} %broadcast_add_fusion.2), kind=kOutput, calls=%fused_computation.109 | convolution fusion | flops 1616248832 | bytes 3950592 | tf_op jit(solution)/shard_map/dot_general | solution.py:221
  141.6 1.3 collective-permute-start.32
  142.9 1.3 collective-permute-start.38
  144.3 2.2 %collective-permute-done.34 = bf16[1024,256]{1,0:T(8,128)(2,1)S(1)} collective-permute-done((bf16[1024,256]{1,0:T(8,128)(2,1)S(1)}, bf16[1024,256]{1,0:T(8,128)(2,1)S(1)}, u32[]{:S(2)}, u32[]{:S(2)}) %collective-permute-start.34) | collective-permute-done | bytes 524320 | tf_op jit(solution)/shard_map/ppermute | solution.py:20
  147.3 3.2 %fusion.82 = bf16[1024,384]{1,0:T(8,128)(2,1)} fusion(bf16[2048,384]{0,1:T(8,128)(2,1)S(1)} %maximum_maximum_fusion, bf16[2048,384]{0,1:T(8,128)(2,1)S(1)} %constant_dynamic-update-slice_fusion.9, f32[2048]{0:T(1024)S(1)} %broadcast_multiply_fusion, pred[2048]{0:T(1024)(128)(4,1)S(1)} %get-tuple-element.138, s32[2048]{0:T(1024)S(1)} %get-tuple-element.140), kind=kOutput, calls=%fused_computation.108 | convolution fusion | flops 1616248832 | bytes 3950592 | tf_op jit(solution)/shard_map/dot_general | solution.py:221
  150.6 2.4 %fusion.88 = bf16[1024,384]{1,0:T(8,128)(2,1)S(1)} fusion(bf16[2048,384]{0,1:T(8,128)(2,1)S(1)} %maximum_maximum_fusion, bf16[2048,384]{0,1:T(8,128)(2,1)S(1)} %constant_dynamic-update-slice_fusion.9, f32[2048]{0:T(1024)S(1)} %broadcast_multiply_fusion.2, pred[2048]{0:T(1024)(128)(4,1)S(1)} %get-tuple-element.139, s32[2048]{0:T(1024)S(1)} %get-tuple-element.141), kind=kOutput, calls=%fused_computation.110 | convolution fusion | flops 1616248832 | bytes 3950592 | tf_op jit(solution)/shard_map/dot_general | solution.py:221
  152.9 10.4 %collective-permute-done.38 = bf16[1024,384]{1,0:T(8,128)(2,1)S(1)} collective-permute-done((bf16[1024,384]{1,0:T(8,128)(2,1)S(1)}, bf16[1024,384]{1,0:T(8,128)(2,1)S(1)}, u32[]{:S(2)}, u32[]{:S(2)}) %collective-permute-start.38) | collective-permute-done | bytes 786464 | tf_op jit(solution)/shard_map/ppermute | solution.py:20
  163.4 1.1 add_convert_fusion
  164.4 1.6 collective-permute-start.43
  166.0 1.1 add_convert_fusion.1
  167.1 4.1 %collective-permute-start.42 = (bf16[1024,384]{1,0:T(8,128)(2,1)}, bf16[1024,384]{1,0:T(8,128)(2,1)}, u32[]{:S(2)}, u32[]{:S(2)}) collective-permute-start(bf16[1024,384]{1,0:T(8,128)(2,1)} %add_convert_fusion.1), channel_id=1, source_target_pairs={{0,2},{1,3},{2,0},{3,1},{4,6},{5,7},{6,4},{7,5},{8,10},{9,11},{10,... | collective-permute-start | bytes 2359304 | tf_op jit(solution)/shard_map/ppermute | solution.py:20
  171.6 5.5 %collective-permute-start.41 = (bf16[256,384]{0,1:T(8,128)(2,1)S(1)}, bf16[256,384]{0,1:T(8,128)(2,1)S(1)}, u32[]{:S(2)}, u32[]{:S(2)}) collective-permute-start(bf16[256,384]{0,1:T(8,128)(2,1)S(1)} %get-tuple-element.93), channel_id=1, source_target_pairs={{0,24},{8,16},{16,8},{24,0},{1,25},{9,17},{17,9},{25,1},{2,26},{10... | collective-permute-start | bytes 589832 | tf_op jit(solution)/shard_map/ppermute | solution.py:34
  177.6 1.3 collective-permute-start.40
  180.5 1.5 collective-permute-done.41
  182.0 1.4 fusion.179
  183.5 3.6 %collective-permute-done.40 = bf16[256,384]{0,1:T(8,128)(2,1)S(1)} collective-permute-done((bf16[256,384]{0,1:T(8,128)(2,1)S(1)}, bf16[256,384]{0,1:T(8,128)(2,1)S(1)}, u32[]{:S(2)}, u32[]{:S(2)}) %collective-permute-start.40) | collective-permute-done | bytes 196640 | tf_op jit(solution)/shard_map/ppermute | solution.py:34
  187.1 1.4 fusion.103
  188.9 1.4 fusion.104
  192.6 3.0 %convert_add_fusion = f32[1024,384]{1,0:T(8,128)} fusion(bf16[1024,384]{1,0:T(8,128)(2,1)} %collective-permute-done.43, bf16[1024,384]{1,0:T(8,128)(2,1)} %collective-permute-done.42, bf16[1024,384]{1,0:T(8,128)(2,1)} %fusion.82), kind=kLoop, calls=%fused_computation.97 | loop fusion | flops 1966080 | bytes 3932160 | tf_op jit(solution)/shard_map/add | solution.py:241
  (163 shorter events, 23.1 us)
Async XLA Ops:
  0.6 1.9 copy-start
  0.6 7.5 %copy-start.15 = (s32[256,4]{0,1:T(4,128)S(1)}, s32[256,4]{0,1:T(4,128)}, u32[]{:S(2)}) copy-start(s32[256,4]{0,1:T(4,128)} %param.7) | copy-start | bytes 12292
  0.7 7.5 %copy-start.16 = (s32[256,4]{0,1:T(4,128)S(1)}, s32[256,4]{0,1:T(4,128)}, u32[]{:S(2)}) copy-start(s32[256,4]{0,1:T(4,128)} %param.6) | copy-start | bytes 12292
  2.6 8.3 %collective-permute-start = (bf16[1024,128]{1,0:T(8,128)(2,1)S(1)}, bf16[1024,128]{1,0:T(8,128)(2,1)}, u32[]{:S(2)}, u32[]{:S(2)}) collective-permute-start(bf16[1024,128]{1,0:T(8,128)(2,1)S(1)} %constant_dynamic-slice_fusion.1), channel_id=1, source_target_pairs={{0,2},{1,3},{2,0},{3,1},{4,6},{5,7},{6,4},{7,5},{8,10},{9,11},{10,... | collective-permute-start | bytes 786440 | tf_op jit(solution)/shard_map/ppermute | solution.py:20
  5.6 28.9 %collective-permute-start.9 = (bf16[1024,256]{1,0:T(8,128)(2,1)}, bf16[1024,256]{1,0:T(8,128)(2,1)}, u32[]{:S(2)}, u32[]{:S(2)}) collective-permute-start(bf16[1024,256]{1,0:T(8,128)(2,1)} %constant_dynamic-slice_fusion), channel_id=1, source_target_pairs={{0,2},{1,3},{2,0},{3,1},{4,6},{5,7},{6,4},{7,5},{8,10},{9,11},{10,... | collective-permute-start | bytes 1572872 | tf_op jit(solution)/shard_map/ppermute | solution.py:20
  6.6 25.3 %collective-permute-start.7 = (bf16[1024,384]{1,0:T(8,128)(2,1)}, bf16[1024,384]{1,0:T(8,128)(2,1)}, u32[]{:S(2)}, u32[]{:S(2)}) collective-permute-start(bf16[1024,384]{1,0:T(8,128)(2,1)} %constant_dynamic-slice_fusion.14), channel_id=1, source_target_pairs={{2,4},{3,5},{4,2},{5,3},{10,12},{11,13},{12,10},{13,11},{18,20},{1... | collective-permute-start | bytes 2359304 | tf_op jit(solution)/shard_map/ppermute | solution.py:20
  10.9 7.7 %collective-permute-start.2 = (s32[4,256]{1,0:T(4,128)S(1)}, s32[4,256]{1,0:T(4,128)S(1)}, u32[]{:S(2)}, u32[]{:S(2)}) collective-permute-start(s32[4,256]{1,0:T(4,128)S(1)} %add_bitcast_fusion), channel_id=1, source_target_pairs={{0,16},{8,24},{16,0},{24,8},{1,17},{9,25},{17,1},{25,9},{2,18},{10... | collective-permute-start | bytes 12296 | tf_op jit(solution)/shard_map/ppermute | solution.py:34
  12.0 8.0 %collective-permute-start.1 = (s32[4,256]{1,0:T(4,128)S(1)}, s32[4,256]{1,0:T(4,128)S(1)}, u32[]{:S(2)}, u32[]{:S(2)}) collective-permute-start(s32[4,256]{1,0:T(4,128)S(1)} %add_bitcast_fusion), channel_id=1, source_target_pairs={{0,8},{8,0},{16,24},{24,16},{1,9},{9,1},{17,25},{25,17},{2,10},{10... | collective-permute-start | bytes 12296 | tf_op jit(solution)/shard_map/ppermute | solution.py:34
  18.5 11.0 %collective-permute-start.12 = (bf16[256,384]{0,1:T(8,128)(2,1)S(1)}, bf16[256,384]{0,1:T(8,128)(2,1)S(1)}, u32[]{:S(2)}, u32[]{:S(2)}) collective-permute-start(bf16[256,384]{0,1:T(8,128)(2,1)S(1)} %get-tuple-element.96), channel_id=1, source_target_pairs={{0,24},{8,16},{16,8},{24,0},{1,25},{9,17},{17,9},{25,1},{2,26},{10... | collective-permute-start | bytes 589832 | tf_op jit(solution)/shard_map/ppermute | solution.py:34
  18.6 11.8 %collective-permute-start.11 = (bf16[256,384]{0,1:T(8,128)(2,1)S(1)}, bf16[256,384]{0,1:T(8,128)(2,1)S(1)}, u32[]{:S(2)}, u32[]{:S(2)}) collective-permute-start(bf16[256,384]{0,1:T(8,128)(2,1)S(1)} %get-tuple-element.97), channel_id=1, source_target_pairs={{0,16},{8,24},{16,0},{24,8},{1,17},{9,25},{17,1},{25,9},{2,18},{10... | collective-permute-start | bytes 589832 | tf_op jit(solution)/shard_map/ppermute | solution.py:34
  20.0 1.6 collective-permute-start.3
  21.6 2.9 %collective-permute-start.4 = (s32[4,1024]{1,0:T(4,128)S(1)}, s32[4,1024]{1,0:T(4,128)S(1)}, u32[]{:S(2)}, u32[]{:S(2)}) collective-permute-start(s32[4,1024]{1,0:T(4,128)S(1)} %pad_add_fusion), channel_id=1, source_target_pairs={{0,1},{1,0},{2,3},{3,2},{4,5},{5,4},{6,7},{7,6},{8,9},{9,8},{10,11... | collective-permute-start | bytes 49160 | tf_op jit(solution)/shard_map/ppermute | solution.py:29
  24.5 6.0 %collective-permute-start.10 = (bf16[256,384]{0,1:T(8,128)(2,1)S(1)}, bf16[256,384]{0,1:T(8,128)(2,1)S(1)}, u32[]{:S(2)}, u32[]{:S(2)}) collective-permute-start(bf16[256,384]{0,1:T(8,128)(2,1)S(1)} %get-tuple-element.98), channel_id=1, source_target_pairs={{0,8},{8,0},{16,24},{24,16},{1,9},{9,1},{17,25},{25,17},{2,10},{10... | collective-permute-start | bytes 589832 | tf_op jit(solution)/shard_map/ppermute | solution.py:34
  29.6 5.7 %copy-start.2 = (bf16[256,1536]{1,0:T(8,128)(2,1)S(1)}, bf16[256,1536]{1,0:T(8,128)(2,1)}, u32[]{:S(2)}) copy-start(bf16[256,1536]{1,0:T(8,128)(2,1)} %param.4) | copy-start | bytes 2359300
  29.6 3.6 %collective-permute-start.5 = (bf16[1024,128]{1,0:T(8,128)(2,1)}, bf16[1024,128]{1,0:T(8,128)(2,1)S(1)}, u32[]{:S(2)}, u32[]{:S(2)}) collective-permute-start(bf16[1024,128]{1,0:T(8,128)(2,1)} %collective-permute-done), channel_id=1, source_target_pairs={{2,4},{3,5},{4,2},{5,3},{10,12},{11,13},{12,10},{13,11},{18,20},{1... | collective-permute-start | bytes 786440 | tf_op jit(solution)/shard_map/ppermute | solution.py:20
  30.5 19.2 %collective-permute-start.26 = (bf16[1024,384]{0,1:T(8,128)(2,1)S(1)}, bf16[1024,384]{0,1:T(8,128)(2,1)S(1)}, u32[]{:S(2)}, u32[]{:S(2)}) collective-permute-start(bf16[1024,384]{0,1:T(8,128)(2,1)S(1)} %pad_maximum_fusion), channel_id=1, source_target_pairs={{0,1},{1,0},{2,3},{3,2},{4,5},{5,4},{6,7},{7,6},{8,9},{9,8},{10,11... | collective-permute-start | bytes 2359304 | tf_op jit(solution)/shard_map/ppermute | solution.py:29
  31.8 22.7 %collective-permute-start.8 = (bf16[1024,384]{1,0:T(8,128)(2,1)}, bf16[1024,384]{1,0:T(8,128)(2,1)S(1)}, u32[]{:S(2)}, u32[]{:S(2)}) collective-permute-start(bf16[1024,384]{1,0:T(8,128)(2,1)} %collective-permute-done.7), channel_id=1, source_target_pairs={{2,0},{3,1},{4,6},{5,7},{10,8},{11,9},{12,14},{13,15},{18,16},{19,... | collective-permute-start | bytes 2359304 | tf_op jit(solution)/shard_map/ppermute | solution.py:20
  33.2 27.3 %collective-permute-start.6 = (bf16[1024,128]{1,0:T(8,128)(2,1)S(1)}, bf16[1024,128]{1,0:T(8,128)(2,1)S(1)}, u32[]{:S(2)}, u32[]{:S(2)}) collective-permute-start(bf16[1024,128]{1,0:T(8,128)(2,1)S(1)} %collective-permute-done.5), channel_id=1, source_target_pairs={{2,0},{3,1},{4,6},{5,7},{10,8},{11,9},{12,14},{13,15},{18,16},{19,... | collective-permute-start | bytes 786440 | tf_op jit(solution)/shard_map/ppermute | solution.py:20
  34.5 22.7 %collective-permute-start.20 = (bf16[1024,256]{1,0:T(8,128)(2,1)}, bf16[1024,256]{1,0:T(8,128)(2,1)S(1)}, u32[]{:S(2)}, u32[]{:S(2)}) collective-permute-start(bf16[1024,256]{1,0:T(8,128)(2,1)} %collective-permute-done.9), channel_id=1, source_target_pairs={{2,4},{3,5},{4,2},{5,3},{10,12},{11,13},{12,10},{13,11},{18,20},{1... | collective-permute-start | bytes 1572872 | tf_op jit(solution)/shard_map/ppermute | solution.py:20
  35.3 23.3 %collective-permute-start.13 = (bf16[256,1536]{1,0:T(8,128)(2,1)S(1)}, bf16[256,1536]{1,0:T(8,128)(2,1)S(1)}, u32[]{:S(2)}, u32[]{:S(2)}) collective-permute-start(bf16[256,1536]{1,0:T(8,128)(2,1)S(1)} %copy-done.2), channel_id=1, source_target_pairs={{0,16},{8,24},{16,0},{24,8},{1,17},{9,25},{17,1},{25,9},{2,18},{10... | collective-permute-start | bytes 2359304 | tf_op jit(solution)/shard_map/ppermute | solution.py:34
  57.2 15.0 %collective-permute-start.21 = (bf16[1024,256]{1,0:T(8,128)(2,1)S(1)}, bf16[1024,256]{1,0:T(8,128)(2,1)S(1)}, u32[]{:S(2)}, u32[]{:S(2)}) collective-permute-start(bf16[1024,256]{1,0:T(8,128)(2,1)S(1)} %collective-permute-done.20), channel_id=1, source_target_pairs={{2,0},{3,1},{4,6},{5,7},{10,8},{11,9},{12,14},{13,15},{18,16},{19,... | collective-permute-start | bytes 1572872 | tf_op jit(solution)/shard_map/ppermute | solution.py:20
  58.6 29.4 %collective-permute-start.18 = (bf16[256,1536]{1,0:T(8,128)(2,1)S(1)}, bf16[256,1536]{1,0:T(8,128)(2,1)S(1)}, u32[]{:S(2)}, u32[]{:S(2)}) collective-permute-start(bf16[256,1536]{1,0:T(8,128)(2,1)S(1)} %copy-done.2), channel_id=1, source_target_pairs={{0,8},{8,0},{16,24},{24,16},{1,9},{9,1},{17,25},{25,17},{2,10},{10... | collective-permute-start | bytes 2359304 | tf_op jit(solution)/shard_map/ppermute | solution.py:34
  60.4 31.7 %collective-permute-start.19 = (bf16[256,1536]{1,0:T(8,128)(2,1)S(1)}, bf16[256,1536]{1,0:T(8,128)(2,1)S(1)}, u32[]{:S(2)}, u32[]{:S(2)}) collective-permute-start(bf16[256,1536]{1,0:T(8,128)(2,1)S(1)} %collective-permute-done.13), channel_id=1, source_target_pairs={{0,8},{8,0},{16,24},{24,16},{1,9},{9,1},{17,25},{25,17},{2,10},{10... | collective-permute-start | bytes 2359304 | tf_op jit(solution)/shard_map/ppermute | solution.py:34
  62.8 7.2 %collective-permute-start.14 = (bf16[1024,128]{0,1:T(8,128)(2,1)S(1)}, bf16[1024,128]{0,1:T(8,128)(2,1)S(1)}, u32[]{:S(2)}, u32[]{:S(2)}) collective-permute-start(bf16[1024,128]{0,1:T(8,128)(2,1)S(1)} %get-tuple-element.39), channel_id=1, source_target_pairs={{0,1},{1,0},{2,3},{3,2},{4,5},{5,4},{6,7},{7,6},{8,9},{9,8},{10,11... | collective-permute-start | bytes 786440 | tf_op jit(solution)/shard_map/ppermute | solution.py:29
  70.0 6.2 %collective-permute-start.16 = (bf16[1024,128]{0,1:T(8,128)(2,1)S(1)}, bf16[1024,128]{0,1:T(8,128)(2,1)S(1)}, u32[]{:S(2)}, u32[]{:S(2)}) collective-permute-start(bf16[1024,128]{0,1:T(8,128)(2,1)S(1)} %add.198), channel_id=1, source_target_pairs={{0,16},{8,24},{16,0},{24,8},{1,17},{9,25},{17,1},{25,9},{2,18},{10... | collective-permute-start | bytes 786440 | tf_op jit(solution)/shard_map/ppermute | solution.py:34
  70.3 16.2 %collective-permute-start.15 = (bf16[1024,128]{0,1:T(8,128)(2,1)S(1)}, bf16[1024,128]{0,1:T(8,128)(2,1)S(1)}, u32[]{:S(2)}, u32[]{:S(2)}) collective-permute-start(bf16[1024,128]{0,1:T(8,128)(2,1)S(1)} %add.198), channel_id=1, source_target_pairs={{0,8},{8,0},{16,24},{24,16},{1,9},{9,1},{17,25},{25,17},{2,10},{10... | collective-permute-start | bytes 786440 | tf_op jit(solution)/shard_map/ppermute | solution.py:34
  76.3 2.6 %collective-permute-start.27 = (f32[4,1024]{1,0:T(4,128)S(1)}, f32[4,1024]{1,0:T(4,128)S(1)}, u32[]{:S(2)}, u32[]{:S(2)}) collective-permute-start(f32[4,1024]{1,0:T(4,128)S(1)} %slice.338), channel_id=1, source_target_pairs={{0,1},{1,0},{2,3},{3,2},{4,5},{5,4},{6,7},{7,6},{8,9},{9,8},{10,11... | collective-permute-start | bytes 49160 | tf_op jit(solution)/shard_map/ppermute | solution.py:29
  76.6 11.5 %collective-permute-start.22 = (bf16[1024,256]{0,1:T(8,128)(2,1)S(1)}, bf16[1024,256]{0,1:T(8,128)(2,1)S(1)}, u32[]{:S(2)}, u32[]{:S(2)}) collective-permute-start(bf16[1024,256]{0,1:T(8,128)(2,1)S(1)} %get-tuple-element.49), channel_id=1, source_target_pairs={{0,1},{1,0},{2,3},{3,2},{4,5},{5,4},{6,7},{7,6},{8,9},{9,8},{10,11... | collective-permute-start | bytes 1572872 | tf_op jit(solution)/shard_map/ppermute | solution.py:29
  78.9 2.6 %collective-permute-start.28 = (f32[4,1024]{1,0:T(4,128)S(1)}, f32[4,1024]{1,0:T(4,128)S(1)}, u32[]{:S(2)}, u32[]{:S(2)}) collective-permute-start(f32[4,1024]{1,0:T(4,128)S(1)} %slice_add_fusion.1), channel_id=1, source_target_pairs={{0,16},{8,24},{16,0},{24,8},{1,17},{9,25},{17,1},{25,9},{2,18},{10... | collective-permute-start | bytes 49160 | tf_op jit(solution)/shard_map/ppermute | solution.py:34
  81.4 6.4 %collective-permute-start.17 = (bf16[1024,128]{0,1:T(8,128)(2,1)S(1)}, bf16[1024,128]{0,1:T(8,128)(2,1)S(1)}, u32[]{:S(2)}, u32[]{:S(2)}) collective-permute-start(bf16[1024,128]{0,1:T(8,128)(2,1)S(1)} %collective-permute-done.16), channel_id=1, source_target_pairs={{0,8},{8,0},{16,24},{24,16},{1,9},{9,1},{17,25},{25,17},{2,10},{10... | collective-permute-start | bytes 786440 | tf_op jit(solution)/shard_map/ppermute | solution.py:34
  86.5 1.2 collective-permute-start.29
  86.7 20.0 %copy-start.3 = (bf16[256,128]{0,1:T(8,128)(2,1)}, bf16[256,128]{0,1:T(8,128)(2,1)S(1)}, u32[]{:S(2)}) copy-start(bf16[256,128]{0,1:T(8,128)(2,1)S(1)} %get-tuple-element.111) | copy-start | bytes 196612
  86.7 20.0 %copy-start.5 = (bf16[256,128]{0,1:T(8,128)(2,1)}, bf16[256,128]{0,1:T(8,128)(2,1)S(1)}, u32[]{:S(2)}) copy-start(bf16[256,128]{0,1:T(8,128)(2,1)S(1)} %get-tuple-element.112) | copy-start | bytes 196612
  86.7 20.0 %copy-start.7 = (bf16[256,128]{0,1:T(8,128)(2,1)}, bf16[256,128]{0,1:T(8,128)(2,1)S(1)}, u32[]{:S(2)}) copy-start(bf16[256,128]{0,1:T(8,128)(2,1)S(1)} %get-tuple-element.113) | copy-start | bytes 196612
  86.7 20.0 %copy-start.9 = (bf16[256,128]{0,1:T(8,128)(2,1)}, bf16[256,128]{0,1:T(8,128)(2,1)S(1)}, u32[]{:S(2)}) copy-start(bf16[256,128]{0,1:T(8,128)(2,1)S(1)} %get-tuple-element.114) | copy-start | bytes 196612
  87.9 18.7 %copy-start.11 = (bf16[256,128]{0,1:T(8,128)(2,1)}, bf16[256,128]{0,1:T(8,128)(2,1)S(1)}, u32[]{:S(2)}) copy-start(bf16[256,128]{0,1:T(8,128)(2,1)S(1)} %get-tuple-element.119) | copy-start | bytes 196612
  87.9 18.7 %copy-start.13 = (bf16[256,128]{0,1:T(8,128)(2,1)}, bf16[256,128]{0,1:T(8,128)(2,1)S(1)}, u32[]{:S(2)}) copy-start(bf16[256,128]{0,1:T(8,128)(2,1)S(1)} %get-tuple-element.120) | copy-start | bytes 196612
  88.2 10.4 %collective-permute-start.24 = (bf16[1024,256]{0,1:T(8,128)(2,1)S(1)}, bf16[1024,256]{0,1:T(8,128)(2,1)S(1)}, u32[]{:S(2)}, u32[]{:S(2)}) collective-permute-start(bf16[1024,256]{0,1:T(8,128)(2,1)S(1)} %add.199), channel_id=1, source_target_pairs={{0,16},{8,24},{16,0},{24,8},{1,17},{9,25},{17,1},{25,9},{2,18},{10... | collective-permute-start | bytes 1572872 | tf_op jit(solution)/shard_map/ppermute | solution.py:34
  88.6 14.3 %collective-permute-start.23 = (bf16[1024,256]{0,1:T(8,128)(2,1)S(1)}, bf16[1024,256]{0,1:T(8,128)(2,1)S(1)}, u32[]{:S(2)}, u32[]{:S(2)}) collective-permute-start(bf16[1024,256]{0,1:T(8,128)(2,1)S(1)} %add.199), channel_id=1, source_target_pairs={{0,8},{8,0},{16,24},{24,16},{1,9},{9,1},{17,25},{25,17},{2,10},{10... | collective-permute-start | bytes 1572872 | tf_op jit(solution)/shard_map/ppermute | solution.py:34
  98.6 5.6 %collective-permute-start.25 = (bf16[1024,256]{0,1:T(8,128)(2,1)S(1)}, bf16[1024,256]{0,1:T(8,128)(2,1)S(1)}, u32[]{:S(2)}, u32[]{:S(2)}) collective-permute-start(bf16[1024,256]{0,1:T(8,128)(2,1)S(1)} %collective-permute-done.24), channel_id=1, source_target_pairs={{0,8},{8,0},{16,24},{24,16},{1,9},{9,1},{17,25},{25,17},{2,10},{10... | collective-permute-start | bytes 1572872 | tf_op jit(solution)/shard_map/ppermute | solution.py:34
  108.3 68.7 %copy-start.17 = (bf16[1024,1024]{1,0:T(8,128)(2,1)}, bf16[1024,1024]{1,0:T(8,128)(2,1)S(1)}, u32[]{:S(2)}) copy-start(bf16[1024,1024]{1,0:T(8,128)(2,1)S(1)} %get-tuple-element.77) | copy-start | bytes 6291460
  108.4 3.3 %collective-permute-start.30 = (f32[8,1024]{1,0:T(8,128)S(1)}, f32[8,1024]{1,0:T(8,128)S(1)}, u32[]{:S(2)}, u32[]{:S(2)}) collective-permute-start(f32[8,1024]{1,0:T(8,128)S(1)} %pad_maximum_fusion.1), channel_id=1, source_target_pairs={{0,1},{1,0},{2,3},{3,2},{4,5},{5,4},{6,7},{7,6},{8,9},{9,8},{10,11... | collective-permute-start | bytes 98312 | tf_op jit(solution)/shard_map/ppermute | solution.py:29
  111.0 7.3 %collective-permute-start.33 = (bf16[1024,128]{0,1:T(8,128)(2,1)S(1)}, bf16[1024,128]{0,1:T(8,128)(2,1)S(1)}, u32[]{:S(2)}, u32[]{:S(2)}) collective-permute-start(bf16[1024,128]{0,1:T(8,128)(2,1)S(1)} %slice.351), channel_id=1, source_target_pairs={{0,1},{1,0},{2,3},{3,2},{4,5},{5,4},{6,7},{7,6},{8,9},{9,8},{10,11... | collective-permute-start | bytes 786440 | tf_op jit(solution)/shard_map/ppermute | solution.py:29
  111.7 20.1 %collective-permute-start.31 = (bf16[1024,256]{0,1:T(8,128)(2,1)S(1)}, bf16[1024,256]{0,1:T(8,128)(2,1)S(1)}, u32[]{:S(2)}, u32[]{:S(2)}) collective-permute-start(bf16[1024,256]{0,1:T(8,128)(2,1)S(1)} %slice.350), channel_id=1, source_target_pairs={{0,1},{1,0},{2,3},{3,2},{4,5},{5,4},{6,7},{7,6},{8,9},{9,8},{10,11... | collective-permute-start | bytes 1572872 | tf_op jit(solution)/shard_map/ppermute | solution.py:29
  119.8 11.1 %collective-permute-start.35 = (bf16[1024,128]{1,0:T(8,128)(2,1)S(1)}, bf16[1024,128]{1,0:T(8,128)(2,1)S(1)}, u32[]{:S(2)}, u32[]{:S(2)}) collective-permute-start(bf16[1024,128]{1,0:T(8,128)(2,1)S(1)} %fusion.92), channel_id=1, source_target_pairs={{0,2},{1,3},{6,4},{7,5},{8,10},{9,11},{14,12},{15,13},{16,18},{17,... | collective-permute-start | bytes 786440 | tf_op jit(solution)/shard_map/ppermute | solution.py:20
  131.0 35.0 %collective-permute-start.36 = (bf16[1024,128]{1,0:T(8,128)(2,1)S(1)}, bf16[1024,128]{1,0:T(8,128)(2,1)S(1)}, u32[]{:S(2)}, u32[]{:S(2)}) collective-permute-start(bf16[1024,128]{1,0:T(8,128)(2,1)S(1)} %add_convert_fusion.3), channel_id=1, source_target_pairs={{2,4},{3,5},{4,2},{5,3},{10,12},{11,13},{12,10},{13,11},{18,20},{1... | collective-permute-start | bytes 786440 | tf_op jit(solution)/shard_map/ppermute | solution.py:20
  133.6 12.9 %collective-permute-start.34 = (bf16[1024,256]{1,0:T(8,128)(2,1)S(1)}, bf16[1024,256]{1,0:T(8,128)(2,1)S(1)}, u32[]{:S(2)}, u32[]{:S(2)}) collective-permute-start(bf16[1024,256]{1,0:T(8,128)(2,1)S(1)} %fusion.91), channel_id=1, source_target_pairs={{0,2},{1,3},{6,4},{7,5},{8,10},{9,11},{14,12},{15,13},{16,18},{17,... | collective-permute-start | bytes 1572872 | tf_op jit(solution)/shard_map/ppermute | solution.py:20
  141.6 29.6 %collective-permute-start.32 = (bf16[1024,384]{0,1:T(8,128)(2,1)S(1)}, bf16[1024,384]{0,1:T(8,128)(2,1)S(1)}, u32[]{:S(2)}, u32[]{:S(2)}) collective-permute-start(bf16[1024,384]{0,1:T(8,128)(2,1)S(1)} %slice.395), channel_id=1, source_target_pairs={{0,1},{1,0},{2,3},{3,2},{4,5},{5,4},{6,7},{7,6},{8,9},{9,8},{10,11... | collective-permute-start | bytes 2359304 | tf_op jit(solution)/shard_map/ppermute | solution.py:29
  142.9 20.4 %collective-permute-start.38 = (bf16[1024,384]{1,0:T(8,128)(2,1)S(1)}, bf16[1024,384]{1,0:T(8,128)(2,1)S(1)}, u32[]{:S(2)}, u32[]{:S(2)}) collective-permute-start(bf16[1024,384]{1,0:T(8,128)(2,1)S(1)} %fusion.85), channel_id=1, source_target_pairs={{0,2},{1,3},{6,4},{7,5},{8,10},{9,11},{14,12},{15,13},{16,18},{17,... | collective-permute-start | bytes 2359304 | tf_op jit(solution)/shard_map/ppermute | solution.py:20
  146.6 19.4 %collective-permute-start.37 = (bf16[1024,256]{1,0:T(8,128)(2,1)S(1)}, bf16[1024,256]{1,0:T(8,128)(2,1)S(1)}, u32[]{:S(2)}, u32[]{:S(2)}) collective-permute-start(bf16[1024,256]{1,0:T(8,128)(2,1)S(1)} %add_convert_fusion.2), channel_id=1, source_target_pairs={{2,4},{3,5},{4,2},{5,3},{10,12},{11,13},{12,10},{13,11},{18,20},{1... | collective-permute-start | bytes 1572872 | tf_op jit(solution)/shard_map/ppermute | solution.py:20
  164.4 28.2 %collective-permute-start.43 = (bf16[1024,384]{1,0:T(8,128)(2,1)}, bf16[1024,384]{1,0:T(8,128)(2,1)}, u32[]{:S(2)}, u32[]{:S(2)}) collective-permute-start(bf16[1024,384]{1,0:T(8,128)(2,1)} %add_convert_fusion), channel_id=1, source_target_pairs={{2,4},{3,5},{4,2},{5,3},{10,12},{11,13},{12,10},{13,11},{18,20},{1... | collective-permute-start | bytes 2359304 | tf_op jit(solution)/shard_map/ppermute | solution.py:20
  167.1 25.5 %collective-permute-start.42 = (bf16[1024,384]{1,0:T(8,128)(2,1)}, bf16[1024,384]{1,0:T(8,128)(2,1)}, u32[]{:S(2)}, u32[]{:S(2)}) collective-permute-start(bf16[1024,384]{1,0:T(8,128)(2,1)} %add_convert_fusion.1), channel_id=1, source_target_pairs={{0,2},{1,3},{2,0},{3,1},{4,6},{5,7},{6,4},{7,5},{8,10},{9,11},{10,... | collective-permute-start | bytes 2359304 | tf_op jit(solution)/shard_map/ppermute | solution.py:20
  171.6 10.4 %collective-permute-start.41 = (bf16[256,384]{0,1:T(8,128)(2,1)S(1)}, bf16[256,384]{0,1:T(8,128)(2,1)S(1)}, u32[]{:S(2)}, u32[]{:S(2)}) collective-permute-start(bf16[256,384]{0,1:T(8,128)(2,1)S(1)} %get-tuple-element.93), channel_id=1, source_target_pairs={{0,24},{8,16},{16,8},{24,0},{1,25},{9,17},{17,9},{25,1},{2,26},{10... | collective-permute-start | bytes 589832 | tf_op jit(solution)/shard_map/ppermute | solution.py:34
  177.1 5.0 %copy-start.12 = (bf16[256,128]{0,1:T(8,128)(2,1)S(1)}, bf16[256,128]{0,1:T(8,128)(2,1)}, u32[]{:S(2)}) copy-start(bf16[256,128]{0,1:T(8,128)(2,1)} %copy-done.11) | copy-start | bytes 196612
  177.1 5.0 %copy-start.14 = (bf16[256,128]{0,1:T(8,128)(2,1)S(1)}, bf16[256,128]{0,1:T(8,128)(2,1)}, u32[]{:S(2)}) copy-start(bf16[256,128]{0,1:T(8,128)(2,1)} %copy-done.13) | copy-start | bytes 196612
  177.6 9.5 %collective-permute-start.40 = (bf16[256,384]{0,1:T(8,128)(2,1)S(1)}, bf16[256,384]{0,1:T(8,128)(2,1)S(1)}, u32[]{:S(2)}, u32[]{:S(2)}) collective-permute-start(bf16[256,384]{0,1:T(8,128)(2,1)S(1)} %get-tuple-element.94), channel_id=1, source_target_pairs={{0,16},{8,24},{16,0},{24,8},{1,17},{9,25},{17,1},{25,9},{2,18},{10... | collective-permute-start | bytes 589832 | tf_op jit(solution)/shard_map/ppermute | solution.py:34
  178.9 10.0 %collective-permute-start.39 = (bf16[256,384]{0,1:T(8,128)(2,1)S(1)}, bf16[256,384]{0,1:T(8,128)(2,1)S(1)}, u32[]{:S(2)}, u32[]{:S(2)}) collective-permute-start(bf16[256,384]{0,1:T(8,128)(2,1)S(1)} %get-tuple-element.95), channel_id=1, source_target_pairs={{0,8},{8,0},{16,24},{24,16},{1,9},{9,1},{17,25},{25,17},{2,10},{10... | collective-permute-start | bytes 589832 | tf_op jit(solution)/shard_map/ppermute | solution.py:34
  183.4 5.5 %copy-start.4 = (bf16[256,128]{0,1:T(8,128)(2,1)S(1)}, bf16[256,128]{0,1:T(8,128)(2,1)}, u32[]{:S(2)}) copy-start(bf16[256,128]{0,1:T(8,128)(2,1)} %copy-done.3) | copy-start | bytes 196612
  183.5 5.5 %copy-start.6 = (bf16[256,128]{0,1:T(8,128)(2,1)S(1)}, bf16[256,128]{0,1:T(8,128)(2,1)}, u32[]{:S(2)}) copy-start(bf16[256,128]{0,1:T(8,128)(2,1)} %copy-done.5) | copy-start | bytes 196612
  183.5 5.5 %copy-start.8 = (bf16[256,128]{0,1:T(8,128)(2,1)S(1)}, bf16[256,128]{0,1:T(8,128)(2,1)}, u32[]{:S(2)}) copy-start(bf16[256,128]{0,1:T(8,128)(2,1)} %copy-done.7) | copy-start | bytes 196612
  183.5 5.5 %copy-start.10 = (bf16[256,128]{0,1:T(8,128)(2,1)S(1)}, bf16[256,128]{0,1:T(8,128)(2,1)}, u32[]{:S(2)}) copy-start(bf16[256,128]{0,1:T(8,128)(2,1)} %copy-done.9) | copy-start | bytes 196612
  191.2 4.4 %copy-start.1 = (bf16[1024,1536]{1,0:T(8,128)(2,1)S(1)}, bf16[1024,1536]{1,0:T(8,128)(2,1)}, u32[]{:S(2)}) copy-start(bf16[1024,1536]{1,0:T(8,128)(2,1)} %param.5) | copy-start | bytes 9437188
where the time goes:
time: 196 us
  starting transfers between devices  71.2 us (36%)
  waiting for transfers between devices  62.4 us (32%)
  matrix products  35.3 us (18%)
  local copies, waits for them, and re-layouts  14.3 us (7%)
  other arithmetic  10.8 us (6%)
    ppermute x20, starting transfers between devices, across(): return lax.ppermute(value, 'blk', [(b, b ^ bit) for b in range(size)])  32.1 us
    ppermute x15, starting transfers between devices, line_permute(): return lax.ppermute(value, 'corpus', full)  31.1 us
    ppermute x9, waiting for transfers between devices, beside(): return lax.ppermute(value, 'corpus', [(c, c ^ 1) for c in range(size)])  22.7 us
    ppermute x15, waiting for transfers between devices, line_permute(): return lax.ppermute(value, 'corpus', full)  22 us
    ppermute x20, waiting for transfers between devices, across(): return lax.ppermute(value, 'blk', [(b, b ^ bit) for b in range(size)])  17.7 us
    dot_general x5, matrix products, pick(): return jnp.dot(hot, rows, preferred_element_type=f32).astype(bf16)  14.3 us
    dot_general x5, matrix products, share(): return jnp.dot(hot, value, preferred_element_type=f32)  11.2 us
    ppermute x9, starting transfers between devices, beside(): return lax.ppermute(value, 'corpus', [(c, c ^ 1) for c in range(size)])  8.01 us
  transfers between devices with their start and end apart: 44, of which 18 were waited for; matrix products, arithmetic and copies ran while one was open for 26% of the time, Pallas kernels for 0%

commit v1 on v0

--- a/solution.py
+++ b/solution.py
@@ -236,6 +236,7 @@
         beside_sum = (beside_sum.astype(f32) + crossed.astype(f32)).astype(bf16)
         third = (third.astype(f32) + inner.astype(f32)).astype(bf16)
         table_grad = apart(rowwise(share(0, later, wide).astype(bf16))).astype(f32)
+        beside_sum, third = apart((beside_sum, third))
         gate = (beside_sum, third)
         table_grad = table_grad + line_permute(beside_sum, END_SWAP).astype(f32)
         table_grad = table_grad + line_permute(third, MIDDLE_SWAP).astype(f32)

time: 196 us -> 194 us (0.990)
  starting transfers between devices: 71.2 us -> 69 us
  transfers between devices with their start and end apart: 44 -> 44, of which waited for: 18 -> 18; matrix products, arithmetic and copies ran while one was open for 26% -> 27% of each run, Pallas kernels for 0% -> 0%
where the time goes in v1:
time: 194 us; the launch traced here: 193 us
  starting transfers between devices  69 us (36%)
  waiting for transfers between devices  62.4 us (32%)
  matrix products  35.3 us (18%)
  local copies, waits for them, and re-layouts  14.3 us (7%)
  other arithmetic  10.9 us (6%)
    ppermute x20, starting transfers between devices, across(): return lax.ppermute(value, 'blk', [(b, b ^ bit) for b in range(size)])  31.8 us
    ppermute x15, starting transfers between devices, line_permute(): return lax.ppermute(value, 'corpus', full)  29.1 us
    ppermute x9, waiting for transfers between devices, beside(): return lax.ppermute(value, 'corpus', [(c, c ^ 1) for c in range(size)])  22.7 us
    ppermute x15, waiting for transfers between devices, line_permute(): return lax.ppermute(value, 'corpus', full)  22 us
    ppermute x20, waiting for transfers between devices, across(): return lax.ppermute(value, 'blk', [(b, b ^ bit) for b in range(size)])  17.7 us
    dot_general x5, matrix products, pick(): return jnp.dot(hot, rows, preferred_element_type=f32).astype(bf16)  14.3 us
    dot_general x5, matrix products, share(): return jnp.dot(hot, value, preferred_element_type=f32)  11.2 us
    ppermute x9, starting transfers between devices, beside(): return lax.ppermute(value, 'corpus', [(c, c ^ 1) for c in range(size)])  8.01 us
  transfers between devices with their start and end apart: 44, of which 18 were waited for; matrix products, arithmetic and copies ran while one was open for 27% of the time, Pallas kernels for 0%

profile of v1, /device:TPU:1, one launch (start us, length us, event | category | flops | bytes accessed | tf_op | source)
XLA Modules:
  0.0 193.4 jit_solution(15787538735872103151)
XLA Ops:
  0.7 1.9 copy-done
  2.6 2.2 %collective-permute-start = (bf16[1024,128]{1,0:T(8,128)(2,1)S(1)}, bf16[1024,128]{1,0:T(8,128)(2,1)}, u32[]{:S(2)}, u32[]{:S(2)}) collective-permute-start(bf16[1024,128]{1,0:T(8,128)(2,1)S(1)} %constant_dynamic-slice_fusion.1), channel_id=1, source_target_pairs={{0,2},{1,3},{2,0},{3,1},{4,6},{5,7},{6,4},{7,5},{8,10},{9,11},{10,... | collective-permute-start | bytes 786440 | tf_op jit(solution)/shard_map/ppermute | solution.py:20
  6.6 1.6 collective-permute-start.7
  8.2 1.2 constant_dynamic-update-slice_fusion.8
  9.4 1.5 collective-permute-done
  10.9 1.1 collective-permute-start.2
  12.0 3.0 %collective-permute-start.1 = (s32[4,256]{1,0:T(4,128)S(1)}, s32[4,256]{1,0:T(4,128)S(1)}, u32[]{:S(2)}, u32[]{:S(2)}) collective-permute-start(s32[4,256]{1,0:T(4,128)S(1)} %add_bitcast_fusion), channel_id=1, source_target_pairs={{0,8},{8,0},{16,24},{24,16},{1,9},{9,1},{17,25},{25,17},{2,10},{10... | collective-permute-start | bytes 12296 | tf_op jit(solution)/shard_map/ppermute | solution.py:34
  15.0 2.3 %copy.7 = bf16[256,1536]{0,1:T(8,128)(2,1)} copy(bf16[256,1536]{1,0:T(8,128)(2,1)} %param.4) | data formatting | bytes 1572864 | tf_op jit(solution)/shard_map/optimization_barrier | solution.py:89
  17.2 1.3 constant_dynamic-update-slice_fusion.13
  18.6 1.3 collective-permute-start.11
  21.6 1.2 collective-permute-start.4
  22.8 1.7 collective-permute-done.4
  24.5 1.2 collective-permute-start.10
  25.9 3.6 %fusion.30 = bf16[2048,384]{0,1:T(8,128)(2,1)S(1)} fusion(bf16[1024,384]{1,0:T(8,128)(2,1)} %constant_dynamic-slice_fusion.14, s32[2048]{0:T(1024)S(1)} %get-tuple-element.144), kind=kOutput, calls=%fused_computation.52 | convolution fusion | flops 1613496320 | bytes 2367488 | tf_op jit(solution)/shard_map/dot_general | solution.py:143
  30.5 1.3 collective-permute-start.26
  31.8 1.3 collective-permute-start.8
  33.2 1.3 collective-permute-start.6
  35.5 3.6 %fusion.31 = bf16[2048,384]{0,1:T(8,128)(2,1)S(1)} fusion(s32[2048]{0:T(1024)S(1)} %get-tuple-element.145, bf16[1024,256]{1,0:T(8,128)(2,1)} %collective-permute-done.9, bf16[1024,128]{1,0:T(8,128)(2,1)} %collective-permute-done), kind=kOutput, calls=%fused_computation.53 | convolution fusion | flops 1615069184 | bytes 2367488 | tf_op jit(solution)/shard_map/dot_general | solution.py:143
  39.1 10.6 %collective-permute-done.26 = bf16[1024,384]{0,1:T(8,128)(2,1)S(1)} collective-permute-done((bf16[1024,384]{0,1:T(8,128)(2,1)S(1)}, bf16[1024,384]{0,1:T(8,128)(2,1)S(1)}, u32[]{:S(2)}, u32[]{:S(2)}) %collective-permute-start.26) | collective-permute-done | bytes 786464 | tf_op jit(solution)/shard_map/ppermute | solution.py:29
  49.8 4.7 %collective-permute-done.8 = bf16[1024,384]{1,0:T(8,128)(2,1)S(1)} collective-permute-done((bf16[1024,384]{1,0:T(8,128)(2,1)}, bf16[1024,384]{1,0:T(8,128)(2,1)S(1)}, u32[]{:S(2)}, u32[]{:S(2)}) %collective-permute-start.8) | collective-permute-done | bytes 786464 | tf_op jit(solution)/shard_map/ppermute | solution.py:20
  54.5 2.5 %select_select_fusion = (bf16[2048,384]{0,1:T(8,128)(2,1)S(1)}, bf16[2048,384]{0,1:T(8,128)(2,1)S(1)}) fusion(bf16[2048,384]{0,1:T(8,128)(2,1)S(1)} %fusion.31, bf16[2048,384]{0,1:T(8,128)(2,1)S(1)} %fusion.30, pred[2048]{0:T(1024)(128)(4,1)S(1)} %get-tuple-element.142, pred[2048]{0:T(1024)(128)(4,1)S(1)} %get-tuple-element.143, ...), kind=kOutput, calls=%fused_computation.104 | convolution fusion | flops 1616248832 | bytes 7878657 | tf_op jit(solution)/shard_map/dot_general | solution.py:143
  57.2 1.3 collective-permute-start.21
  58.6 1.9 collective-permute-start.18
  60.5 2.1 %fusion.34 = bf16[2048,128]{0,1:T(8,128)(2,1)S(1)} fusion(s32[2048]{0:T(1024)S(1)} %broadcast_add_fusion.3, bf16[1024,128]{1,0:T(8,128)(2,1)S(1)} %collective-permute-done.5, bf16[1024,128]{1,0:T(8,128)(2,1)S(1)} %collective-permute-done.6, pred[]{:T(512)S(6)} %or.3), kind=kOutput, calls=%fused_computation.56 | convolution fusion | flops 539361280 | bytes 1056769 | tf_op jit(solution)/shard_map/dot_general | solution.py:143
  63.1 1.4 fusion.24
  64.6 5.3 %collective-permute-done.14 = bf16[1024,128]{0,1:T(8,128)(2,1)S(1)} collective-permute-done((bf16[1024,128]{0,1:T(8,128)(2,1)S(1)}, bf16[1024,128]{0,1:T(8,128)(2,1)S(1)}, u32[]{:S(2)}, u32[]{:S(2)}) %collective-permute-start.14) | collective-permute-done | bytes 262176 | tf_op jit(solution)/shard_map/ppermute | solution.py:29
  70.3 1.9 collective-permute-start.15
  72.2 2.5 %fusion.33 = bf16[2048,256]{0,1:T(8,128)(2,1)S(1)} fusion(s32[2048]{0:T(1024)S(1)} %broadcast_add_fusion.3, bf16[1024,256]{1,0:T(8,128)(2,1)S(1)} %collective-permute-done.20, bf16[1024,256]{1,0:T(8,128)(2,1)S(1)} %collective-permute-done.21, pred[]{:T(512)S(6)} %or.3), kind=kOutput, calls=%fused_computation.55 | convolution fusion | flops 1076625408 | bytes 2105345 | tf_op jit(solution)/shard_map/dot_general | solution.py:143
  76.6 1.3 collective-permute-start.22
  79.2 2.2 %collective-permute-done.28 = f32[4,1024]{1,0:T(4,128)S(1)} collective-permute-done((f32[4,1024]{1,0:T(4,128)S(1)}, f32[4,1024]{1,0:T(4,128)S(1)}, u32[]{:S(2)}, u32[]{:S(2)}) %collective-permute-start.28) | collective-permute-done | bytes 16416 | tf_op jit(solution)/shard_map/ppermute | solution.py:34
  81.4 5.1 %collective-permute-start.17 = (bf16[1024,128]{0,1:T(8,128)(2,1)S(1)}, bf16[1024,128]{0,1:T(8,128)(2,1)S(1)}, u32[]{:S(2)}, u32[]{:S(2)}) collective-permute-start(bf16[1024,128]{0,1:T(8,128)(2,1)S(1)} %collective-permute-done.16), channel_id=1, source_target_pairs={{0,8},{8,0},{16,24},{24,16},{1,9},{9,1},{17,25},{25,17},{2,10},{10... | collective-permute-start | bytes 786440 | tf_op jit(solution)/shard_map/ppermute | solution.py:34
  86.7 1.1 collective-permute-done.29
  88.6 3.6 %collective-permute-start.23 = (bf16[1024,256]{0,1:T(8,128)(2,1)S(1)}, bf16[1024,256]{0,1:T(8,128)(2,1)S(1)}, u32[]{:S(2)}, u32[]{:S(2)}) collective-permute-start(bf16[1024,256]{0,1:T(8,128)(2,1)S(1)} %add.199), channel_id=1, source_target_pairs={{0,8},{8,0},{16,24},{24,16},{1,9},{9,1},{17,25},{25,17},{2,10},{10... | collective-permute-start | bytes 1572872 | tf_op jit(solution)/shard_map/ppermute | solution.py:34
  92.4 6.2 %collective-permute-done.24 = bf16[1024,256]{0,1:T(8,128)(2,1)S(1)} collective-permute-done((bf16[1024,256]{0,1:T(8,128)(2,1)S(1)}, bf16[1024,256]{0,1:T(8,128)(2,1)S(1)}, u32[]{:S(2)}, u32[]{:S(2)}) %collective-permute-start.24) | collective-permute-done | bytes 524320 | tf_op jit(solution)/shard_map/ppermute | solution.py:34
  98.6 4.0 %collective-permute-start.25 = (bf16[1024,256]{0,1:T(8,128)(2,1)S(1)}, bf16[1024,256]{0,1:T(8,128)(2,1)S(1)}, u32[]{:S(2)}, u32[]{:S(2)}) collective-permute-start(bf16[1024,256]{0,1:T(8,128)(2,1)S(1)} %collective-permute-done.24), channel_id=1, source_target_pairs={{0,8},{8,0},{16,24},{24,16},{1,9},{9,1},{17,25},{25,17},{2,10},{10... | collective-permute-start | bytes 1572872 | tf_op jit(solution)/shard_map/ppermute | solution.py:34
  102.9 1.3 collective-permute-done.25
  104.2 2.4 %fusion.36 = f32[1024,1024]{1,0:T(8,128)S(1)} fusion(bf16[256,256]{0,1:T(8,128)(2,1)S(1)} %get-tuple-element.110, bf16[256,256]{0,1:T(8,128)(2,1)S(1)} %get-tuple-element.111, bf16[256,256]{0,1:T(8,128)(2,1)S(1)} %get-tuple-element.112, bf16[256,256]{0,1:T(8,128)(2,1)S(1)} %get-tuple-element.109, bf16[512,256]{0,1:T(8,128)(2,1)S(1)} %get-tuple-element.108, ...), kind=kOutput, calls=%fused_computation.59 | convolution fusion | flops 2178940928 | bytes 8388608 | tf_op jit(solution)/shard_map/dot_general | solution.py:197
  106.7 1.7 convert_reduce_fusion
  112.7 1.4 fusion.23
  114.1 4.1 %collective-permute-done.33 = bf16[1024,128]{0,1:T(8,128)(2,1)S(1)} collective-permute-done((bf16[1024,128]{0,1:T(8,128)(2,1)S(1)}, bf16[1024,128]{0,1:T(8,128)(2,1)S(1)}, u32[]{:S(2)}, u32[]{:S(2)}) %collective-permute-start.33) | collective-permute-done | bytes 262176 | tf_op jit(solution)/shard_map/ppermute | solution.py:29
  118.3 1.6 fusion.92
  119.8 7.8 %collective-permute-start.35 = (bf16[1024,128]{1,0:T(8,128)(2,1)S(1)}, bf16[1024,128]{1,0:T(8,128)(2,1)S(1)}, u32[]{:S(2)}, u32[]{:S(2)}) collective-permute-start(bf16[1024,128]{1,0:T(8,128)(2,1)S(1)} %fusion.92), channel_id=1, source_target_pairs={{0,2},{1,3},{6,4},{7,5},{8,10},{9,11},{14,12},{15,13},{16,18},{17,... | collective-permute-start | bytes 786440 | tf_op jit(solution)/shard_map/ppermute | solution.py:20
  127.8 3.1 %collective-permute-done.35 = bf16[1024,128]{1,0:T(8,128)(2,1)S(1)} collective-permute-done((bf16[1024,128]{1,0:T(8,128)(2,1)S(1)}, bf16[1024,128]{1,0:T(8,128)(2,1)S(1)}, u32[]{:S(2)}, u32[]{:S(2)}) %collective-permute-start.35) | collective-permute-done | bytes 262176 | tf_op jit(solution)/shard_map/ppermute | solution.py:20
  131.9 1.7 fusion.91
  133.6 5.5 %collective-permute-start.34 = (bf16[1024,256]{1,0:T(8,128)(2,1)S(1)}, bf16[1024,256]{1,0:T(8,128)(2,1)S(1)}, u32[]{:S(2)}, u32[]{:S(2)}) collective-permute-start(bf16[1024,256]{1,0:T(8,128)(2,1)S(1)} %fusion.91), channel_id=1, source_target_pairs={{0,2},{1,3},{6,4},{7,5},{8,10},{9,11},{14,12},{15,13},{16,18},{17,... | collective-permute-start | bytes 1572872 | tf_op jit(solution)/shard_map/ppermute | solution.py:20
  139.3 2.4 %fusion.85 = bf16[1024,384]{1,0:T(8,128)(2,1)S(1)} fusion(bf16[2048,384]{0,1:T(8,128)(2,1)S(1)} %maximum_maximum_fusion, bf16[2048,384]{0,1:T(8,128)(2,1)S(1)} %constant_dynamic-update-slice_fusion.9, f32[2048]{0:T(1024)S(1)} %broadcast_multiply_fusion.1, pred[2048]{0:T(1024)(128)(4,1)S(1)} %slice_reduce_fusion.2, s32[2048]{0:T(1024)S(1)} %broadcast_add_fusion.2), kind=kOutput, calls=%fused_computation.109 | convolution fusion | flops 1616248832 | bytes 3950592 | tf_op jit(solution)/shard_map/dot_general | solution.py:221
  141.6 1.3 collective-permute-start.32
  142.9 1.3 collective-permute-start.38
  144.3 2.2 %collective-permute-done.34 = bf16[1024,256]{1,0:T(8,128)(2,1)S(1)} collective-permute-done((bf16[1024,256]{1,0:T(8,128)(2,1)S(1)}, bf16[1024,256]{1,0:T(8,128)(2,1)S(1)}, u32[]{:S(2)}, u32[]{:S(2)}) %collective-permute-start.34) | collective-permute-done | bytes 524320 | tf_op jit(solution)/shard_map/ppermute | solution.py:20
  147.4 3.3 %fusion.82 = bf16[1024,384]{1,0:T(8,128)(2,1)} fusion(bf16[2048,384]{0,1:T(8,128)(2,1)S(1)} %maximum_maximum_fusion, bf16[2048,384]{0,1:T(8,128)(2,1)S(1)} %constant_dynamic-update-slice_fusion.9, f32[2048]{0:T(1024)S(1)} %broadcast_multiply_fusion, pred[2048]{0:T(1024)(128)(4,1)S(1)} %get-tuple-element.142, s32[2048]{0:T(1024)S(1)} %get-tuple-element.144), kind=kOutput, calls=%fused_computation.108 | convolution fusion | flops 1616248832 | bytes 3950592 | tf_op jit(solution)/shard_map/dot_general | solution.py:221
  150.6 2.4 %fusion.88 = bf16[1024,384]{1,0:T(8,128)(2,1)S(1)} fusion(bf16[2048,384]{0,1:T(8,128)(2,1)S(1)} %maximum_maximum_fusion, bf16[2048,384]{0,1:T(8,128)(2,1)S(1)} %constant_dynamic-update-slice_fusion.9, f32[2048]{0:T(1024)S(1)} %broadcast_multiply_fusion.2, pred[2048]{0:T(1024)(128)(4,1)S(1)} %get-tuple-element.143, s32[2048]{0:T(1024)S(1)} %get-tuple-element.145), kind=kOutput, calls=%fused_computation.110 | convolution fusion | flops 1616248832 | bytes 3950592 | tf_op jit(solution)/shard_map/dot_general | solution.py:221
  153.0 10.4 %collective-permute-done.38 = bf16[1024,384]{1,0:T(8,128)(2,1)S(1)} collective-permute-done((bf16[1024,384]{1,0:T(8,128)(2,1)S(1)}, bf16[1024,384]{1,0:T(8,128)(2,1)S(1)}, u32[]{:S(2)}, u32[]{:S(2)}) %collective-permute-start.38) | collective-permute-done | bytes 786464 | tf_op jit(solution)/shard_map/ppermute | solution.py:20
  163.4 1.1 add_convert_fusion
  164.5 1.1 add_convert_fusion.1
  165.6 2.2 %collective-permute-start.42 = (bf16[1024,384]{1,0:T(8,128)(2,1)}, bf16[1024,384]{1,0:T(8,128)(2,1)}, u32[]{:S(2)}, u32[]{:S(2)}) collective-permute-start(bf16[1024,384]{1,0:T(8,128)(2,1)} %add_convert_fusion.1), channel_id=1, source_target_pairs={{0,2},{1,3},{2,0},{3,1},{4,6},{5,7},{6,4},{7,5},{8,10},{9,11},{10,... | collective-permute-start | bytes 2359304 | tf_op jit(solution)/shard_map/ppermute | solution.py:20
  167.8 1.5 collective-permute-start.43
  169.7 5.2 %collective-permute-start.41 = (bf16[256,384]{0,1:T(8,128)(2,1)S(1)}, bf16[256,384]{0,1:T(8,128)(2,1)S(1)}, u32[]{:S(2)}, u32[]{:S(2)}) collective-permute-start(bf16[256,384]{0,1:T(8,128)(2,1)S(1)} %get-tuple-element.97), channel_id=1, source_target_pairs={{0,24},{8,16},{16,8},{24,0},{1,25},{9,17},{17,9},{25,1},{2,26},{10... | collective-permute-start | bytes 589832 | tf_op jit(solution)/shard_map/ppermute | solution.py:34
  175.4 1.3 collective-permute-start.40
  178.3 1.5 collective-permute-done.41
  179.8 1.4 fusion.179
  181.3 3.6 %collective-permute-done.40 = bf16[256,384]{0,1:T(8,128)(2,1)S(1)} collective-permute-done((bf16[256,384]{0,1:T(8,128)(2,1)S(1)}, bf16[256,384]{0,1:T(8,128)(2,1)S(1)}, u32[]{:S(2)}, u32[]{:S(2)}) %collective-permute-start.40) | collective-permute-done | bytes 196640 | tf_op jit(solution)/shard_map/ppermute | solution.py:34
  184.9 1.4 fusion.103
  186.7 1.4 fusion.104
  190.4 3.0 %convert_add_fusion = f32[1024,384]{1,0:T(8,128)} fusion(bf16[1024,384]{1,0:T(8,128)(2,1)} %collective-permute-done.43, bf16[1024,384]{1,0:T(8,128)(2,1)} %collective-permute-done.42, bf16[1024,384]{1,0:T(8,128)(2,1)} %fusion.82), kind=kLoop, calls=%fused_computation.97 | loop fusion | flops 1966080 | bytes 3932160 | tf_op jit(solution)/shard_map/add | solution.py:242
  (163 shorter events, 23.1 us)
Async XLA Ops:
  0.6 1.9 copy-start
  0.6 7.5 %copy-start.15 = (s32[256,4]{0,1:T(4,128)S(1)}, s32[256,4]{0,1:T(4,128)}, u32[]{:S(2)}) copy-start(s32[256,4]{0,1:T(4,128)} %param.7) | copy-start | bytes 12292
  0.7 7.5 %copy-start.16 = (s32[256,4]{0,1:T(4,128)S(1)}, s32[256,4]{0,1:T(4,128)}, u32[]{:S(2)}) copy-start(s32[256,4]{0,1:T(4,128)} %param.6) | copy-start | bytes 12292
  2.6 8.3 %collective-permute-start = (bf16[1024,128]{1,0:T(8,128)(2,1)S(1)}, bf16[1024,128]{1,0:T(8,128)(2,1)}, u32[]{:S(2)}, u32[]{:S(2)}) collective-permute-start(bf16[1024,128]{1,0:T(8,128)(2,1)S(1)} %constant_dynamic-slice_fusion.1), channel_id=1, source_target_pairs={{0,2},{1,3},{2,0},{3,1},{4,6},{5,7},{6,4},{7,5},{8,10},{9,11},{10,... | collective-permute-start | bytes 786440 | tf_op jit(solution)/shard_map/ppermute | solution.py:20
  5.6 28.9 %collective-permute-start.9 = (bf16[1024,256]{1,0:T(8,128)(2,1)}, bf16[1024,256]{1,0:T(8,128)(2,1)}, u32[]{:S(2)}, u32[]{:S(2)}) collective-permute-start(bf16[1024,256]{1,0:T(8,128)(2,1)} %constant_dynamic-slice_fusion), channel_id=1, source_target_pairs={{0,2},{1,3},{2,0},{3,1},{4,6},{5,7},{6,4},{7,5},{8,10},{9,11},{10,... | collective-permute-start | bytes 1572872 | tf_op jit(solution)/shard_map/ppermute | solution.py:20
  6.6 25.3 %collective-permute-start.7 = (bf16[1024,384]{1,0:T(8,128)(2,1)}, bf16[1024,384]{1,0:T(8,128)(2,1)}, u32[]{:S(2)}, u32[]{:S(2)}) collective-permute-start(bf16[1024,384]{1,0:T(8,128)(2,1)} %constant_dynamic-slice_fusion.14), channel_id=1, source_target_pairs={{2,4},{3,5},{4,2},{5,3},{10,12},{11,13},{12,10},{13,11},{18,20},{1... | collective-permute-start | bytes 2359304 | tf_op jit(solution)/shard_map/ppermute | solution.py:20
  10.9 7.7 %collective-permute-start.2 = (s32[4,256]{1,0:T(4,128)S(1)}, s32[4,256]{1,0:T(4,128)S(1)}, u32[]{:S(2)}, u32[]{:S(2)}) collective-permute-start(s32[4,256]{1,0:T(4,128)S(1)} %add_bitcast_fusion), channel_id=1, source_target_pairs={{0,16},{8,24},{16,0},{24,8},{1,17},{9,25},{17,1},{25,9},{2,18},{10... | collective-permute-start | bytes 12296 | tf_op jit(solution)/shard_map/ppermute | solution.py:34
  12.0 8.0 %collective-permute-start.1 = (s32[4,256]{1,0:T(4,128)S(1)}, s32[4,256]{1,0:T(4,128)S(1)}, u32[]{:S(2)}, u32[]{:S(2)}) collective-permute-start(s32[4,256]{1,0:T(4,128)S(1)} %add_bitcast_fusion), channel_id=1, source_target_pairs={{0,8},{8,0},{16,24},{24,16},{1,9},{9,1},{17,25},{25,17},{2,10},{10... | collective-permute-start | bytes 12296 | tf_op jit(solution)/shard_map/ppermute | solution.py:34
  18.5 11.0 %collective-permute-start.12 = (bf16[256,384]{0,1:T(8,128)(2,1)S(1)}, bf16[256,384]{0,1:T(8,128)(2,1)S(1)}, u32[]{:S(2)}, u32[]{:S(2)}) collective-permute-start(bf16[256,384]{0,1:T(8,128)(2,1)S(1)} %get-tuple-element.100), channel_id=1, source_target_pairs={{0,24},{8,16},{16,8},{24,0},{1,25},{9,17},{17,9},{25,1},{2,26},{10... | collective-permute-start | bytes 589832 | tf_op jit(solution)/shard_map/ppermute | solution.py:34
  18.6 11.8 %collective-permute-start.11 = (bf16[256,384]{0,1:T(8,128)(2,1)S(1)}, bf16[256,384]{0,1:T(8,128)(2,1)S(1)}, u32[]{:S(2)}, u32[]{:S(2)}) collective-permute-start(bf16[256,384]{0,1:T(8,128)(2,1)S(1)} %get-tuple-element.101), channel_id=1, source_target_pairs={{0,16},{8,24},{16,0},{24,8},{1,17},{9,25},{17,1},{25,9},{2,18},{10... | collective-permute-start | bytes 589832 | tf_op jit(solution)/shard_map/ppermute | solution.py:34
  20.0 1.6 collective-permute-start.3
  21.6 2.9 %collective-permute-start.4 = (s32[4,1024]{1,0:T(4,128)S(1)}, s32[4,1024]{1,0:T(4,128)S(1)}, u32[]{:S(2)}, u32[]{:S(2)}) collective-permute-start(s32[4,1024]{1,0:T(4,128)S(1)} %pad_add_fusion), channel_id=1, source_target_pairs={{0,1},{1,0},{2,3},{3,2},{4,5},{5,4},{6,7},{7,6},{8,9},{9,8},{10,11... | collective-permute-start | bytes 49160 | tf_op jit(solution)/shard_map/ppermute | solution.py:29
  24.5 6.0 %collective-permute-start.10 = (bf16[256,384]{0,1:T(8,128)(2,1)S(1)}, bf16[256,384]{0,1:T(8,128)(2,1)S(1)}, u32[]{:S(2)}, u32[]{:S(2)}) collective-permute-start(bf16[256,384]{0,1:T(8,128)(2,1)S(1)} %get-tuple-element.102), channel_id=1, source_target_pairs={{0,8},{8,0},{16,24},{24,16},{1,9},{9,1},{17,25},{25,17},{2,10},{10... | collective-permute-start | bytes 589832 | tf_op jit(solution)/shard_map/ppermute | solution.py:34
  29.6 5.7 %copy-start.2 = (bf16[256,1536]{1,0:T(8,128)(2,1)S(1)}, bf16[256,1536]{1,0:T(8,128)(2,1)}, u32[]{:S(2)}) copy-start(bf16[256,1536]{1,0:T(8,128)(2,1)} %param.4) | copy-start | bytes 2359300
  29.6 3.6 %collective-permute-start.5 = (bf16[1024,128]{1,0:T(8,128)(2,1)}, bf16[1024,128]{1,0:T(8,128)(2,1)S(1)}, u32[]{:S(2)}, u32[]{:S(2)}) collective-permute-start(bf16[1024,128]{1,0:T(8,128)(2,1)} %collective-permute-done), channel_id=1, source_target_pairs={{2,4},{3,5},{4,2},{5,3},{10,12},{11,13},{12,10},{13,11},{18,20},{1... | collective-permute-start | bytes 786440 | tf_op jit(solution)/shard_map/ppermute | solution.py:20
  30.5 19.2 %collective-permute-start.26 = (bf16[1024,384]{0,1:T(8,128)(2,1)S(1)}, bf16[1024,384]{0,1:T(8,128)(2,1)S(1)}, u32[]{:S(2)}, u32[]{:S(2)}) collective-permute-start(bf16[1024,384]{0,1:T(8,128)(2,1)S(1)} %pad_maximum_fusion), channel_id=1, source_target_pairs={{0,1},{1,0},{2,3},{3,2},{4,5},{5,4},{6,7},{7,6},{8,9},{9,8},{10,11... | collective-permute-start | bytes 2359304 | tf_op jit(solution)/shard_map/ppermute | solution.py:29
  31.8 22.7 %collective-permute-start.8 = (bf16[1024,384]{1,0:T(8,128)(2,1)}, bf16[1024,384]{1,0:T(8,128)(2,1)S(1)}, u32[]{:S(2)}, u32[]{:S(2)}) collective-permute-start(bf16[1024,384]{1,0:T(8,128)(2,1)} %collective-permute-done.7), channel_id=1, source_target_pairs={{2,0},{3,1},{4,6},{5,7},{10,8},{11,9},{12,14},{13,15},{18,16},{19,... | collective-permute-start | bytes 2359304 | tf_op jit(solution)/shard_map/ppermute | solution.py:20
  33.2 27.3 %collective-permute-start.6 = (bf16[1024,128]{1,0:T(8,128)(2,1)S(1)}, bf16[1024,128]{1,0:T(8,128)(2,1)S(1)}, u32[]{:S(2)}, u32[]{:S(2)}) collective-permute-start(bf16[1024,128]{1,0:T(8,128)(2,1)S(1)} %collective-permute-done.5), channel_id=1, source_target_pairs={{2,0},{3,1},{4,6},{5,7},{10,8},{11,9},{12,14},{13,15},{18,16},{19,... | collective-permute-start | bytes 786440 | tf_op jit(solution)/shard_map/ppermute | solution.py:20
  34.5 22.7 %collective-permute-start.20 = (bf16[1024,256]{1,0:T(8,128)(2,1)}, bf16[1024,256]{1,0:T(8,128)(2,1)S(1)}, u32[]{:S(2)}, u32[]{:S(2)}) collective-permute-start(bf16[1024,256]{1,0:T(8,128)(2,1)} %collective-permute-done.9), channel_id=1, source_target_pairs={{2,4},{3,5},{4,2},{5,3},{10,12},{11,13},{12,10},{13,11},{18,20},{1... | collective-permute-start | bytes 1572872 | tf_op jit(solution)/shard_map/ppermute | solution.py:20
  35.3 23.3 %collective-permute-start.13 = (bf16[256,1536]{1,0:T(8,128)(2,1)S(1)}, bf16[256,1536]{1,0:T(8,128)(2,1)S(1)}, u32[]{:S(2)}, u32[]{:S(2)}) collective-permute-start(bf16[256,1536]{1,0:T(8,128)(2,1)S(1)} %copy-done.2), channel_id=1, source_target_pairs={{0,16},{8,24},{16,0},{24,8},{1,17},{9,25},{17,1},{25,9},{2,18},{10... | collective-permute-start | bytes 2359304 | tf_op jit(solution)/shard_map/ppermute | solution.py:34
  57.2 15.0 %collective-permute-start.21 = (bf16[1024,256]{1,0:T(8,128)(2,1)S(1)}, bf16[1024,256]{1,0:T(8,128)(2,1)S(1)}, u32[]{:S(2)}, u32[]{:S(2)}) collective-permute-start(bf16[1024,256]{1,0:T(8,128)(2,1)S(1)} %collective-permute-done.20), channel_id=1, source_target_pairs={{2,0},{3,1},{4,6},{5,7},{10,8},{11,9},{12,14},{13,15},{18,16},{19,... | collective-permute-start | bytes 1572872 | tf_op jit(solution)/shard_map/ppermute | solution.py:20
  58.6 29.4 %collective-permute-start.18 = (bf16[256,1536]{1,0:T(8,128)(2,1)S(1)}, bf16[256,1536]{1,0:T(8,128)(2,1)S(1)}, u32[]{:S(2)}, u32[]{:S(2)}) collective-permute-start(bf16[256,1536]{1,0:T(8,128)(2,1)S(1)} %copy-done.2), channel_id=1, source_target_pairs={{0,8},{8,0},{16,24},{24,16},{1,9},{9,1},{17,25},{25,17},{2,10},{10... | collective-permute-start | bytes 2359304 | tf_op jit(solution)/shard_map/ppermute | solution.py:34
  60.4 31.7 %collective-permute-start.19 = (bf16[256,1536]{1,0:T(8,128)(2,1)S(1)}, bf16[256,1536]{1,0:T(8,128)(2,1)S(1)}, u32[]{:S(2)}, u32[]{:S(2)}) collective-permute-start(bf16[256,1536]{1,0:T(8,128)(2,1)S(1)} %collective-permute-done.13), channel_id=1, source_target_pairs={{0,8},{8,0},{16,24},{24,16},{1,9},{9,1},{17,25},{25,17},{2,10},{10... | collective-permute-start | bytes 2359304 | tf_op jit(solution)/shard_map/ppermute | solution.py:34
  62.8 7.2 %collective-permute-start.14 = (bf16[1024,128]{0,1:T(8,128)(2,1)S(1)}, bf16[1024,128]{0,1:T(8,128)(2,1)S(1)}, u32[]{:S(2)}, u32[]{:S(2)}) collective-permute-start(bf16[1024,128]{0,1:T(8,128)(2,1)S(1)} %get-tuple-element.41), channel_id=1, source_target_pairs={{0,1},{1,0},{2,3},{3,2},{4,5},{5,4},{6,7},{7,6},{8,9},{9,8},{10,11... | collective-permute-start | bytes 786440 | tf_op jit(solution)/shard_map/ppermute | solution.py:29
  70.0 6.2 %collective-permute-start.16 = (bf16[1024,128]{0,1:T(8,128)(2,1)S(1)}, bf16[1024,128]{0,1:T(8,128)(2,1)S(1)}, u32[]{:S(2)}, u32[]{:S(2)}) collective-permute-start(bf16[1024,128]{0,1:T(8,128)(2,1)S(1)} %add.198), channel_id=1, source_target_pairs={{0,16},{8,24},{16,0},{24,8},{1,17},{9,25},{17,1},{25,9},{2,18},{10... | collective-permute-start | bytes 786440 | tf_op jit(solution)/shard_map/ppermute | solution.py:34
  70.3 16.2 %collective-permute-start.15 = (bf16[1024,128]{0,1:T(8,128)(2,1)S(1)}, bf16[1024,128]{0,1:T(8,128)(2,1)S(1)}, u32[]{:S(2)}, u32[]{:S(2)}) collective-permute-start(bf16[1024,128]{0,1:T(8,128)(2,1)S(1)} %add.198), channel_id=1, source_target_pairs={{0,8},{8,0},{16,24},{24,16},{1,9},{9,1},{17,25},{25,17},{2,10},{10... | collective-permute-start | bytes 786440 | tf_op jit(solution)/shard_map/ppermute | solution.py:34
  76.3 2.6 %collective-permute-start.27 = (f32[4,1024]{1,0:T(4,128)S(1)}, f32[4,1024]{1,0:T(4,128)S(1)}, u32[]{:S(2)}, u32[]{:S(2)}) collective-permute-start(f32[4,1024]{1,0:T(4,128)S(1)} %slice.338), channel_id=1, source_target_pairs={{0,1},{1,0},{2,3},{3,2},{4,5},{5,4},{6,7},{7,6},{8,9},{9,8},{10,11... | collective-permute-start | bytes 49160 | tf_op jit(solution)/shard_map/ppermute | solution.py:29
  76.6 11.5 %collective-permute-start.22 = (bf16[1024,256]{0,1:T(8,128)(2,1)S(1)}, bf16[1024,256]{0,1:T(8,128)(2,1)S(1)}, u32[]{:S(2)}, u32[]{:S(2)}) collective-permute-start(bf16[1024,256]{0,1:T(8,128)(2,1)S(1)} %get-tuple-element.51), channel_id=1, source_target_pairs={{0,1},{1,0},{2,3},{3,2},{4,5},{5,4},{6,7},{7,6},{8,9},{9,8},{10,11... | collective-permute-start | bytes 1572872 | tf_op jit(solution)/shard_map/ppermute | solution.py:29
  78.9 2.6 %collective-permute-start.28 = (f32[4,1024]{1,0:T(4,128)S(1)}, f32[4,1024]{1,0:T(4,128)S(1)}, u32[]{:S(2)}, u32[]{:S(2)}) collective-permute-start(f32[4,1024]{1,0:T(4,128)S(1)} %slice_add_fusion.1), channel_id=1, source_target_pairs={{0,16},{8,24},{16,0},{24,8},{1,17},{9,25},{17,1},{25,9},{2,18},{10... | collective-permute-start | bytes 49160 | tf_op jit(solution)/shard_map/ppermute | solution.py:34
  81.4 6.4 %collective-permute-start.17 = (bf16[1024,128]{0,1:T(8,128)(2,1)S(1)}, bf16[1024,128]{0,1:T(8,128)(2,1)S(1)}, u32[]{:S(2)}, u32[]{:S(2)}) collective-permute-start(bf16[1024,128]{0,1:T(8,128)(2,1)S(1)} %collective-permute-done.16), channel_id=1, source_target_pairs={{0,8},{8,0},{16,24},{24,16},{1,9},{9,1},{17,25},{25,17},{2,10},{10... | collective-permute-start | bytes 786440 | tf_op jit(solution)/shard_map/ppermute | solution.py:34
  86.5 1.2 collective-permute-start.29
  86.7 20.0 %copy-start.3 = (bf16[256,128]{0,1:T(8,128)(2,1)}, bf16[256,128]{0,1:T(8,128)(2,1)S(1)}, u32[]{:S(2)}) copy-start(bf16[256,128]{0,1:T(8,128)(2,1)S(1)} %get-tuple-element.115) | copy-start | bytes 196612
  86.7 20.0 %copy-start.5 = (bf16[256,128]{0,1:T(8,128)(2,1)}, bf16[256,128]{0,1:T(8,128)(2,1)S(1)}, u32[]{:S(2)}) copy-start(bf16[256,128]{0,1:T(8,128)(2,1)S(1)} %get-tuple-element.116) | copy-start | bytes 196612
  86.7 20.0 %copy-start.7 = (bf16[256,128]{0,1:T(8,128)(2,1)}, bf16[256,128]{0,1:T(8,128)(2,1)S(1)}, u32[]{:S(2)}) copy-start(bf16[256,128]{0,1:T(8,128)(2,1)S(1)} %get-tuple-element.117) | copy-start | bytes 196612
  86.7 20.0 %copy-start.9 = (bf16[256,128]{0,1:T(8,128)(2,1)}, bf16[256,128]{0,1:T(8,128)(2,1)S(1)}, u32[]{:S(2)}) copy-start(bf16[256,128]{0,1:T(8,128)(2,1)S(1)} %get-tuple-element.118) | copy-start | bytes 196612
  87.9 18.7 %copy-start.11 = (bf16[256,128]{0,1:T(8,128)(2,1)}, bf16[256,128]{0,1:T(8,128)(2,1)S(1)}, u32[]{:S(2)}) copy-start(bf16[256,128]{0,1:T(8,128)(2,1)S(1)} %get-tuple-element.123) | copy-start | bytes 196612
  87.9 18.7 %copy-start.13 = (bf16[256,128]{0,1:T(8,128)(2,1)}, bf16[256,128]{0,1:T(8,128)(2,1)S(1)}, u32[]{:S(2)}) copy-start(bf16[256,128]{0,1:T(8,128)(2,1)S(1)} %get-tuple-element.124) | copy-start | bytes 196612
  88.2 10.4 %collective-permute-start.24 = (bf16[1024,256]{0,1:T(8,128)(2,1)S(1)}, bf16[1024,256]{0,1:T(8,128)(2,1)S(1)}, u32[]{:S(2)}, u32[]{:S(2)}) collective-permute-start(bf16[1024,256]{0,1:T(8,128)(2,1)S(1)} %add.199), channel_id=1, source_target_pairs={{0,16},{8,24},{16,0},{24,8},{1,17},{9,25},{17,1},{25,9},{2,18},{10... | collective-permute-start | bytes 1572872 | tf_op jit(solution)/shard_map/ppermute | solution.py:34
  88.6 14.3 %collective-permute-start.23 = (bf16[1024,256]{0,1:T(8,128)(2,1)S(1)}, bf16[1024,256]{0,1:T(8,128)(2,1)S(1)}, u32[]{:S(2)}, u32[]{:S(2)}) collective-permute-start(bf16[1024,256]{0,1:T(8,128)(2,1)S(1)} %add.199), channel_id=1, source_target_pairs={{0,8},{8,0},{16,24},{24,16},{1,9},{9,1},{17,25},{25,17},{2,10},{10... | collective-permute-start | bytes 1572872 | tf_op jit(solution)/shard_map/ppermute | solution.py:34
  98.6 5.6 %collective-permute-start.25 = (bf16[1024,256]{0,1:T(8,128)(2,1)S(1)}, bf16[1024,256]{0,1:T(8,128)(2,1)S(1)}, u32[]{:S(2)}, u32[]{:S(2)}) collective-permute-start(bf16[1024,256]{0,1:T(8,128)(2,1)S(1)} %collective-permute-done.24), channel_id=1, source_target_pairs={{0,8},{8,0},{16,24},{24,16},{1,9},{9,1},{17,25},{25,17},{2,10},{10... | collective-permute-start | bytes 1572872 | tf_op jit(solution)/shard_map/ppermute | solution.py:34
  108.3 66.5 %copy-start.17 = (bf16[1024,1024]{1,0:T(8,128)(2,1)}, bf16[1024,1024]{1,0:T(8,128)(2,1)S(1)}, u32[]{:S(2)}) copy-start(bf16[1024,1024]{1,0:T(8,128)(2,1)S(1)} %get-tuple-element.81) | copy-start | bytes 6291460
  108.4 3.3 %collective-permute-start.30 = (f32[8,1024]{1,0:T(8,128)S(1)}, f32[8,1024]{1,0:T(8,128)S(1)}, u32[]{:S(2)}, u32[]{:S(2)}) collective-permute-start(f32[8,1024]{1,0:T(8,128)S(1)} %pad_maximum_fusion.1), channel_id=1, source_target_pairs={{0,1},{1,0},{2,3},{3,2},{4,5},{5,4},{6,7},{7,6},{8,9},{9,8},{10,11... | collective-permute-start | bytes 98312 | tf_op jit(solution)/shard_map/ppermute | solution.py:29
  111.0 7.3 %collective-permute-start.33 = (bf16[1024,128]{0,1:T(8,128)(2,1)S(1)}, bf16[1024,128]{0,1:T(8,128)(2,1)S(1)}, u32[]{:S(2)}, u32[]{:S(2)}) collective-permute-start(bf16[1024,128]{0,1:T(8,128)(2,1)S(1)} %slice.351), channel_id=1, source_target_pairs={{0,1},{1,0},{2,3},{3,2},{4,5},{5,4},{6,7},{7,6},{8,9},{9,8},{10,11... | collective-permute-start | bytes 786440 | tf_op jit(solution)/shard_map/ppermute | solution.py:29
  111.7 20.1 %collective-permute-start.31 = (bf16[1024,256]{0,1:T(8,128)(2,1)S(1)}, bf16[1024,256]{0,1:T(8,128)(2,1)S(1)}, u32[]{:S(2)}, u32[]{:S(2)}) collective-permute-start(bf16[1024,256]{0,1:T(8,128)(2,1)S(1)} %slice.350), channel_id=1, source_target_pairs={{0,1},{1,0},{2,3},{3,2},{4,5},{5,4},{6,7},{7,6},{8,9},{9,8},{10,11... | collective-permute-start | bytes 1572872 | tf_op jit(solution)/shard_map/ppermute | solution.py:29
  119.8 11.1 %collective-permute-start.35 = (bf16[1024,128]{1,0:T(8,128)(2,1)S(1)}, bf16[1024,128]{1,0:T(8,128)(2,1)S(1)}, u32[]{:S(2)}, u32[]{:S(2)}) collective-permute-start(bf16[1024,128]{1,0:T(8,128)(2,1)S(1)} %fusion.92), channel_id=1, source_target_pairs={{0,2},{1,3},{6,4},{7,5},{8,10},{9,11},{14,12},{15,13},{16,18},{17,... | collective-permute-start | bytes 786440 | tf_op jit(solution)/shard_map/ppermute | solution.py:20
  131.0 33.5 %collective-permute-start.36 = (bf16[1024,128]{1,0:T(8,128)(2,1)S(1)}, bf16[1024,128]{1,0:T(8,128)(2,1)S(1)}, u32[]{:S(2)}, u32[]{:S(2)}) collective-permute-start(bf16[1024,128]{1,0:T(8,128)(2,1)S(1)} %add_convert_fusion.3), channel_id=1, source_target_pairs={{2,4},{3,5},{4,2},{5,3},{10,12},{11,13},{12,10},{13,11},{18,20},{1... | collective-permute-start | bytes 786440 | tf_op jit(solution)/shard_map/ppermute | solution.py:20
  133.6 12.9 %collective-permute-start.34 = (bf16[1024,256]{1,0:T(8,128)(2,1)S(1)}, bf16[1024,256]{1,0:T(8,128)(2,1)S(1)}, u32[]{:S(2)}, u32[]{:S(2)}) collective-permute-start(bf16[1024,256]{1,0:T(8,128)(2,1)S(1)} %fusion.91), channel_id=1, source_target_pairs={{0,2},{1,3},{6,4},{7,5},{8,10},{9,11},{14,12},{15,13},{16,18},{17,... | collective-permute-start | bytes 1572872 | tf_op jit(solution)/shard_map/ppermute | solution.py:20
  141.6 27.7 %collective-permute-start.32 = (bf16[1024,384]{0,1:T(8,128)(2,1)S(1)}, bf16[1024,384]{0,1:T(8,128)(2,1)S(1)}, u32[]{:S(2)}, u32[]{:S(2)}) collective-permute-start(bf16[1024,384]{0,1:T(8,128)(2,1)S(1)} %slice.395), channel_id=1, source_target_pairs={{0,1},{1,0},{2,3},{3,2},{4,5},{5,4},{6,7},{7,6},{8,9},{9,8},{10,11... | collective-permute-start | bytes 2359304 | tf_op jit(solution)/shard_map/ppermute | solution.py:29
  142.9 20.4 %collective-permute-start.38 = (bf16[1024,384]{1,0:T(8,128)(2,1)S(1)}, bf16[1024,384]{1,0:T(8,128)(2,1)S(1)}, u32[]{:S(2)}, u32[]{:S(2)}) collective-permute-start(bf16[1024,384]{1,0:T(8,128)(2,1)S(1)} %fusion.85), channel_id=1, source_target_pairs={{0,2},{1,3},{6,4},{7,5},{8,10},{9,11},{14,12},{15,13},{16,18},{17,... | collective-permute-start | bytes 2359304 | tf_op jit(solution)/shard_map/ppermute | solution.py:20
  146.7 17.8 %collective-permute-start.37 = (bf16[1024,256]{1,0:T(8,128)(2,1)S(1)}, bf16[1024,256]{1,0:T(8,128)(2,1)S(1)}, u32[]{:S(2)}, u32[]{:S(2)}) collective-permute-start(bf16[1024,256]{1,0:T(8,128)(2,1)S(1)} %add_convert_fusion.2), channel_id=1, source_target_pairs={{2,4},{3,5},{4,2},{5,3},{10,12},{11,13},{12,10},{13,11},{18,20},{1... | collective-permute-start | bytes 1572872 | tf_op jit(solution)/shard_map/ppermute | solution.py:20
  165.6 24.9 %collective-permute-start.42 = (bf16[1024,384]{1,0:T(8,128)(2,1)}, bf16[1024,384]{1,0:T(8,128)(2,1)}, u32[]{:S(2)}, u32[]{:S(2)}) collective-permute-start(bf16[1024,384]{1,0:T(8,128)(2,1)} %add_convert_fusion.1), channel_id=1, source_target_pairs={{0,2},{1,3},{2,0},{3,1},{4,6},{5,7},{6,4},{7,5},{8,10},{9,11},{10,... | collective-permute-start | bytes 2359304 | tf_op jit(solution)/shard_map/ppermute | solution.py:20
  167.8 22.7 %collective-permute-start.43 = (bf16[1024,384]{1,0:T(8,128)(2,1)}, bf16[1024,384]{1,0:T(8,128)(2,1)}, u32[]{:S(2)}, u32[]{:S(2)}) collective-permute-start(bf16[1024,384]{1,0:T(8,128)(2,1)} %add_convert_fusion), channel_id=1, source_target_pairs={{2,4},{3,5},{4,2},{5,3},{10,12},{11,13},{12,10},{13,11},{18,20},{1... | collective-permute-start | bytes 2359304 | tf_op jit(solution)/shard_map/ppermute | solution.py:20
  169.7 10.2 %collective-permute-start.41 = (bf16[256,384]{0,1:T(8,128)(2,1)S(1)}, bf16[256,384]{0,1:T(8,128)(2,1)S(1)}, u32[]{:S(2)}, u32[]{:S(2)}) collective-permute-start(bf16[256,384]{0,1:T(8,128)(2,1)S(1)} %get-tuple-element.97), channel_id=1, source_target_pairs={{0,24},{8,16},{16,8},{24,0},{1,25},{9,17},{17,9},{25,1},{2,26},{10... | collective-permute-start | bytes 589832 | tf_op jit(solution)/shard_map/ppermute | solution.py:34
  174.9 5.0 %copy-start.12 = (bf16[256,128]{0,1:T(8,128)(2,1)S(1)}, bf16[256,128]{0,1:T(8,128)(2,1)}, u32[]{:S(2)}) copy-start(bf16[256,128]{0,1:T(8,128)(2,1)} %copy-done.11) | copy-start | bytes 196612
  174.9 5.0 %copy-start.14 = (bf16[256,128]{0,1:T(8,128)(2,1)S(1)}, bf16[256,128]{0,1:T(8,128)(2,1)}, u32[]{:S(2)}) copy-start(bf16[256,128]{0,1:T(8,128)(2,1)} %copy-done.13) | copy-start | bytes 196612
  175.4 9.5 %collective-permute-start.40 = (bf16[256,384]{0,1:T(8,128)(2,1)S(1)}, bf16[256,384]{0,1:T(8,128)(2,1)S(1)}, u32[]{:S(2)}, u32[]{:S(2)}) collective-permute-start(bf16[256,384]{0,1:T(8,128)(2,1)S(1)} %get-tuple-element.98), channel_id=1, source_target_pairs={{0,16},{8,24},{16,0},{24,8},{1,17},{9,25},{17,1},{25,9},{2,18},{10... | collective-permute-start | bytes 589832 | tf_op jit(solution)/shard_map/ppermute | solution.py:34
  176.7 10.0 %collective-permute-start.39 = (bf16[256,384]{0,1:T(8,128)(2,1)S(1)}, bf16[256,384]{0,1:T(8,128)(2,1)S(1)}, u32[]{:S(2)}, u32[]{:S(2)}) collective-permute-start(bf16[256,384]{0,1:T(8,128)(2,1)S(1)} %get-tuple-element.99), channel_id=1, source_target_pairs={{0,8},{8,0},{16,24},{24,16},{1,9},{9,1},{17,25},{25,17},{2,10},{10... | collective-permute-start | bytes 589832 | tf_op jit(solution)/shard_map/ppermute | solution.py:34
  181.3 5.5 %copy-start.4 = (bf16[256,128]{0,1:T(8,128)(2,1)S(1)}, bf16[256,128]{0,1:T(8,128)(2,1)}, u32[]{:S(2)}) copy-start(bf16[256,128]{0,1:T(8,128)(2,1)} %copy-done.3) | copy-start | bytes 196612
  181.3 5.5 %copy-start.6 = (bf16[256,128]{0,1:T(8,128)(2,1)S(1)}, bf16[256,128]{0,1:T(8,128)(2,1)}, u32[]{:S(2)}) copy-start(bf16[256,128]{0,1:T(8,128)(2,1)} %copy-done.5) | copy-start | bytes 196612
  181.3 5.5 %copy-start.8 = (bf16[256,128]{0,1:T(8,128)(2,1)S(1)}, bf16[256,128]{0,1:T(8,128)(2,1)}, u32[]{:S(2)}) copy-start(bf16[256,128]{0,1:T(8,128)(2,1)} %copy-done.7) | copy-start | bytes 196612
  181.3 5.5 %copy-start.10 = (bf16[256,128]{0,1:T(8,128)(2,1)S(1)}, bf16[256,128]{0,1:T(8,128)(2,1)}, u32[]{:S(2)}) copy-start(bf16[256,128]{0,1:T(8,128)(2,1)} %copy-done.9) | copy-start | bytes 196612
  189.0 4.4 %copy-start.1 = (bf16[1024,1536]{1,0:T(8,128)(2,1)S(1)}, bf16[1024,1536]{1,0:T(8,128)(2,1)}, u32[]{:S(2)}) copy-start(bf16[1024,1536]{1,0:T(8,128)(2,1)} %param.5) | copy-start | bytes 9437188
